TPU v7x, 256 devices: a whole 4x4x8 slice. The times are simulated.
256 devices in a mesh: group: 16 (over z_lo, y), tok: 16 (over z_hi, x, core).
Axes of the slice: x: 4, y: 4, z: 8 (z_hi: 2, z_lo: 4; z = z_hi * 4 + z_lo), core: 2. Of those that a mesh axis runs over, the one named last changes fastest.
Arguments:
- tokens: bfloat16 [131072, 2048], P(('group', 'tok')), may hold values from -94 to 94
- learning_rates: float32 [2, 131072], P(None, 'group'), may hold values from 0.1 to 1
- channel_gains: float32 [2, 5, 2048], P(None, None, 'tok'), may hold values from 0.3 to 3
- fast_init: float32 [2, 3, 16, 128, 128], P(None, None, 'tok'), may hold values from -0.5 to 0.5
- step_size: float32 [2, 16], P(None, 'tok'), may hold values from 0.05 to 1
- update_table: int32 [2, 16], replicated, may hold values 0 or 1
Outputs:
- mixed: bfloat16 [131072, 2048], P(('group', 'tok'))
All inputs are finite; a program needn't handle non-finite values.
Results may differ from a plain program's by a relative error of at most 0.033.
Values may be sent and summed in bfloat16 or wider, within the bound.
No kernel may reach another device: no remote copies, remote signals or barrier semaphores. Data moves between devices by JAX's collectives and lax.ppermute only.
A program may use at most 64 MiB of HBM per device.

v0:
```python
import jax
import jax.numpy as jnp
from jax import lax
from jax.sharding import PartitionSpec as P

NS_STEPS = 5


MUON_A = 3.4445
MUON_B = -4.775
MUON_C = 2.0315
EPSILON = 1e-06


def passed_along(value, axis, by):
    size = lax.axis_size(axis)
    pairs = [(i, i + by) for i in range(size) if 0 <= i + by < size]
    return lax.ppermute(value, axis, pairs)


def orthogonalize(gradient):
    scaling = lax.rsqrt(jnp.sum(gradient * gradient, axis=(-2, -1), keepdims=True) + EPSILON)
    current = gradient * scaling
    for repeat in range(NS_STEPS):
        square = jnp.einsum("...ij,...kj->...ik", current, current, precision=lax.Precision.HIGHEST)
        polynom = MUON_B * square + MUON_C * jnp.einsum(
            "...ij,...jk->...ik", square, square, precision=lax.Precision.HIGHEST
        )
        current = MUON_A * current + jnp.einsum(
            "...ij,...jk->...ik", polynom, current, precision=lax.Precision.HIGHEST
        )
    return current


def layer_group(stream, entering, gain_rows, rates_row, steps_row, update_flag, inverse):
    row_count, channel_count = stream.shape
    heads_n = entering.shape[1]
    head_dim = entering.shape[2]
    normed = stream.astype(jnp.float32) * inverse[:, None] * gain_rows[0]
    queries = (normed * gain_rows[1]).astype(jnp.bfloat16).reshape(row_count, heads_n, head_dim)
    keys_in = (normed * gain_rows[2]).astype(jnp.bfloat16).reshape(row_count, heads_n, head_dim)
    values_in = (normed * gain_rows[3]).astype(jnp.bfloat16).reshape(row_count, heads_n, head_dim)
    rounded = entering.astype(jnp.bfloat16)
    gate_q = jnp.einsum("thi,hij->thj", queries, rounded[0], preferred_element_type=jnp.float32)
    up_q = jnp.einsum("thi,hij->thj", queries, rounded[1], preferred_element_type=jnp.float32)
    hidden_q = (jax.nn.silu(gate_q) * up_q).astype(jnp.bfloat16)
    output = jnp.einsum(
        "thj,hjk->thk", hidden_q, rounded[2], preferred_element_type=jnp.float32
    ).reshape(row_count, channel_count)
    mixed_rows = (stream.astype(jnp.float32) + gain_rows[4] * output).astype(jnp.bfloat16)
    gate_k = jnp.einsum("thi,hij->thj", keys_in, rounded[0], preferred_element_type=jnp.float32)
    up_k = jnp.einsum("thi,hij->thj", keys_in, rounded[1], preferred_element_type=jnp.float32)
    sigmoid_k = jax.nn.sigmoid(gate_k)
    active_k = gate_k * sigmoid_k
    hidden_k = (active_k * up_k).astype(jnp.bfloat16)
    targets = (rates_row[:, None, None] * values_in.astype(jnp.float32)).astype(jnp.bfloat16)
    back_hidden = jnp.einsum(
        "thk,hjk->thj", targets, rounded[2], preferred_element_type=jnp.float32
    )
    back_up = (back_hidden * active_k).astype(jnp.bfloat16)
    back_gate = (back_hidden * up_k * sigmoid_k * (1.0 + gate_k * (1.0 - sigmoid_k))).astype(
        jnp.bfloat16
    )
    grad_gate = jnp.einsum("thi,thj->hij", keys_in, back_gate, preferred_element_type=jnp.float32)
    grad_up = jnp.einsum("thi,thj->hij", keys_in, back_up, preferred_element_type=jnp.float32)
    grad_down = jnp.einsum("thj,thk->hjk", hidden_k, targets, preferred_element_type=jnp.float32)
    direction = orthogonalize(jnp.stack([grad_gate, grad_up, grad_down]))
    moved_state = entering + (update_flag * steps_row)[None, :, None, None] * direction
    norm_before = jnp.sqrt(jnp.sum(entering * entering, axis=2, keepdims=True) + EPSILON)
    norm_after = jnp.sqrt(jnp.sum(moved_state * moved_state, axis=2, keepdims=True) + EPSILON)
    return (mixed_rows, moved_state * (norm_before / norm_after))


def pass_on(outgoing):
    return passed_along(outgoing, "group", 1)


def body(tokens, learning_rates, channel_gains, fast_init, step_size, update_table):
    start_stream = lax.all_to_all(tokens, "tok", split_axis=1, concat_axis=0, tiled=True)
    group_count = lax.axis_size("group")
    group_index = lax.axis_index("group")
    width_all = start_stream.shape[1] * lax.axis_size("tok")
    layer_count = fast_init.shape[0]
    zero_state = jnp.zeros(fast_init.shape[1:], jnp.float32)

    def tick_work(stream, outgoing, layer_now, active, inverse):
        received = pass_on(outgoing)
        initial = lax.dynamic_index_in_dim(fast_init, layer_now, 0, keepdims=False)
        entering = jnp.where(group_index == 0, initial, received)
        gain_rows = lax.dynamic_index_in_dim(channel_gains, layer_now, 0, keepdims=False)
        rates_row = lax.dynamic_index_in_dim(learning_rates, layer_now, 0, keepdims=False)
        steps_row = lax.dynamic_index_in_dim(step_size, layer_now, 0, keepdims=False)
        table_cell = lax.dynamic_slice(
            update_table, (jnp.asarray(layer_now, jnp.int32), group_index), (1, 1)
        )
        update_flag = table_cell[0, 0].astype(jnp.float32)

        def working(operands):
            return layer_group(
                operands[0], operands[1], gain_rows, rates_row, steps_row, update_flag, inverse
            )

        def resting(operands):
            return (operands[0], operands[2])

        return lax.cond(active, working, resting, (stream, entering, outgoing))

    final_stream = start_stream
    for layer_now in range(layer_count):
        widened = final_stream.astype(jnp.float32)
        totals = lax.psum(jnp.sum(widened * widened, axis=1), "tok")
        inverse = lax.rsqrt(totals / width_all + EPSILON)

        def one_tick(tick_index, loop_state):
            stream, outgoing = loop_state
            active = tick_index == group_index
            return tick_work(stream, outgoing, layer_now, active, inverse)

        final_stream, last_state = lax.fori_loop(
            0, group_count, one_tick, (final_stream, zero_state)
        )
    return lax.all_to_all(final_stream, "tok", split_axis=0, concat_axis=1, tiled=True)


def solution(mesh):
    in_specs = (
        P(("group", "tok"), None),
        P(None, "group"),
        P(None, None, "tok"),
        P(None, None, "tok", None, None),
        P(None, "tok"),
        P(),
    )
    out_specs = P(("group", "tok"), None)
    return jax.shard_map(body, mesh=mesh, in_specs=in_specs, out_specs=out_specs, check_vma=False)
```

profile of v0, /device:TPU:120, one launch (start us, length us, event | category | flops | bytes accessed | tf_op | source)
XLA Modules:
  0.0 1390.3 jit_solution(5411178419686325323)
XLA Ops:
  3.5 8.5 all-to-all-start
  14.0 35.7 %all-to-all-done = bf16[512,16,128]{2,0,1:T(8,128)(2,1)} async-done(((bf16[512,16,128]{2,0,1:T(8,128)(2,1)}), bf16[512,16,128]{2,0,1:T(8,128)(2,1)}, u32[]{:S(2)}, u32[]{:S(2)}) %all-to-all-start) | async-done | bytes 2097184 | tf_op jit(solution)/shard_map/all_to_all | solution.py:79
  52.5 87.6 %psum.14 = f32[8192]{0:T(1024)S(1)} all-reduce(f32[8192]{0:T(1024)S(1)} %bitcast.261), channel_id=1, replica_groups=mesh['group'=16,'tok'=16] {'tok'}, use_global_device_ids=true, to_apply=%region_1.0 | all-reduce | flops 8192 | bytes 65536 | tf_op jit(solution)/shard_map/psum | solution.py:111
  140.2 663.9 %while.34 = (s32[]{:T(128)}, bf16[8192,128]{1,0:T(8,128)(2,1)}, f32[3,1,128,128]{3,2,0,1:T(8,128)S(1)}, s32[]{:T(128)}, f32[2,5,128]{2,1,0:T(8,128)S(1)}, /*inde...) while((s32[]{:T(128)}, bf16[8192,128]{1,0:T(8,128)(2,1)}, ...), condition=%wide.region_8.9_spmd, body=%wide.region_2.8_spmd.sunk | while | flops 3632480256 | bytes 94034832 | solution.py:119
  164.1 24.6 %collective-permute-done = f32[3,1,128,128]{3,2,0,1:T(8,128)S(1)} collective-permute-done((f32[3,1,128,128]{3,2,0,1:T(8,128)S(1)}, f32[3,1,128,128]{3,2,0,1:T(8,128)S(1)}, u32[]{:S(2)}, u32[]{:S(2)}) %collective-permute-start) | collective-permute-done | bytes 196640 | tf_op jit(solution)/shard_map/while/body/eval_jaxpr/ppermute | solution.py:18
  190.0 7.5 collective-permute-done
  198.8 8.1 collective-permute-done
  208.2 8.4 collective-permute-done
  217.9 8.4 collective-permute-done
  227.5 9.8 collective-permute-done
  238.7 10.8 collective-permute-done
  250.8 9.7 collective-permute-done
  261.8 9.0 collective-permute-done
  272.1 7.4 collective-permute-done
  280.8 7.6 collective-permute-done
  289.7 8.4 collective-permute-done
  299.4 469.8 %collective-permute-done = f32[3,1,128,128]{3,2,0,1:T(8,128)S(1)} collective-permute-done((f32[3,1,128,128]{3,2,0,1:T(8,128)S(1)}, f32[3,1,128,128]{3,2,0,1:T(8,128)S(1)}, u32[]{:S(2)}, u32[]{:S(2)}) %collective-permute-start) | collective-permute-done | bytes 196640 | tf_op jit(solution)/shard_map/while/body/eval_jaxpr/ppermute | solution.py:18
  769.2 34.9 %conditional.4 = ((bf16[8192,128]{1,0:T(8,128)(2,1)}, f32[3,1,128,128]{3,2,0,1:T(8,128)S(1)})) conditional(s32[]{:T(128)} %convert_element_type.267, (bf16[8192,128]{1,0:T(8,128)(2,1)}, f32[3,1,128,128]{3,2,0,1:T(8,128)S(1)}) %tuple.101, (bf16[8192,128]{1,0:T(8,128)(2,1)}, f32[2,5,128]{2,1,0:T(8,128)S(1)}, pred[]{:T(512)}, ...), branch_computations={%region_3.3_spmd, %region_4.7_spmd} | conditional | flops 3632480256 | bytes 93248136 | solution.py:106
  790.4 7.2 fusion.3
  806.8 84.2 %psum.15 = f32[8192]{0:T(1024)S(1)} all-reduce(f32[8192]{0:T(1024)S(1)} %multiply_reduce_fusion.4), channel_id=1, replica_groups=mesh['group'=16,'tok'=16] {'tok'}, use_global_device_ids=true, to_apply=%region_10.11 | all-reduce | flops 8192 | bytes 65536 | tf_op jit(solution)/shard_map/psum | solution.py:111
  891.0 453.8 %while.35 = (s32[]{:T(128)}, bf16[8192,128]{1,0:T(8,128)(2,1)}, f32[3,1,128,128]{3,2,0,1:T(8,128)S(1)}, s32[]{:T(128)}, f32[2,5,128]{2,1,0:T(8,128)S(1)}, /*inde...) while((s32[]{:T(128)}, bf16[8192,128]{1,0:T(8,128)(2,1)}, ...), condition=%wide.region_17.18_spmd, body=%wide.region_11.17_spmd.sunk | while | flops 3632480256 | bytes 94034832 | solution.py:119
  929.3 7.8 collective-permute-done.1
  938.4 7.8 collective-permute-done.1
  978.4 7.3 collective-permute-done.1
  987.0 9.8 collective-permute-done.1
  998.0 8.6 collective-permute-done.1
  1008.0 7.4 collective-permute-done.1
  1016.7 7.8 collective-permute-done.1
  1025.8 8.4 collective-permute-done.1
  1035.4 273.3 %collective-permute-done.1 = f32[3,1,128,128]{3,2,0,1:T(8,128)S(1)} collective-permute-done((f32[3,1,128,128]{3,2,0,1:T(8,128)S(1)}, f32[3,1,128,128]{3,2,0,1:T(8,128)S(1)}, u32[]{:S(2)}, u32[]{:S(2)}) %collective-permute-start.1) | collective-permute-done | bytes 196640 | tf_op jit(solution)/shard_map/while/body/eval_jaxpr/ppermute | solution.py:18
  1308.7 36.1 %conditional.5 = ((bf16[8192,128]{1,0:T(8,128)(2,1)}, f32[3,1,128,128]{3,2,0,1:T(8,128)S(1)})) conditional(s32[]{:T(128)} %convert_element_type.268, (bf16[8192,128]{1,0:T(8,128)(2,1)}, f32[3,1,128,128]{3,2,0,1:T(8,128)S(1)}) %tuple.104, (bf16[8192,128]{1,0:T(8,128)(2,1)}, f32[2,5,128]{2,1,0:T(8,128)S(1)}, pred[]{:T(512)}, ...), branch_computations={%region_12.12_spmd, %region_13.16_spmd} | conditional | flops 3632480256 | bytes 93248136 | solution.py:106
  1344.8 37.3 %all_to_all.38 = bf16[16,512,128]{2,1,0:T(8,128)(2,1)} all-to-all(bf16[16,512,128]{2,1,0:T(8,128)(2,1)} %bitcast.82), channel_id=1, replica_groups=mesh['group'=16,'tok'=16] {'tok'}, dimensions={0} | all-to-all | bytes 4194304 | tf_op jit(solution)/shard_map/all_to_all | solution.py:122
  (164 shorter events, 185.0 us)
Async XLA Ops:
  3.5 46.3 %all-to-all-start = ((bf16[512,16,128]{2,0,1:T(8,128)(2,1)}), bf16[512,16,128]{2,0,1:T(8,128)(2,1)}, u32[]{:S(2)}, u32[]{:S(2)}) async-start(bf16[512,16,128]{2,0,1:T(8,128)(2,1)} %copy_bitcast_fusion), calls=%async_computation | async-start | bytes 4194304 | tf_op jit(solution)/shard_map/all_to_all | solution.py:79
  140.2 7.6 collective-permute-start
  147.7 7.6 collective-permute-start
  155.3 7.6 collective-permute-start
  162.8 25.9 %collective-permute-start = (f32[3,1,128,128]{3,2,0,1:T(8,128)S(1)}, f32[3,1,128,128]{3,2,0,1:T(8,128)S(1)}, u32[]{:S(2)}, u32[]{:S(2)}) collective-permute-start(f32[3,1,128,128]{3,2,0,1:T(8,128)S(1)} %get-tuple-element.889), channel_id=1, source_target_pairs={{0,16},{16,32},{32,48},{48,64},{64,80},{80,96},{96,112},{112,128},... | collective-permute-start | bytes 589832 | tf_op jit(solution)/shard_map/while/body/eval_jaxpr/ppermute | solution.py:18
  188.7 8.8 collective-permute-start
  197.5 9.4 collective-permute-start
  206.9 9.7 collective-permute-start
  216.6 9.7 collective-permute-start
  226.3 11.1 collective-permute-start
  237.4 12.1 collective-permute-start
  249.5 11.0 collective-permute-start
  260.5 10.3 collective-permute-start
  270.8 8.7 collective-permute-start
  279.5 8.9 collective-permute-start
  288.4 9.7 collective-permute-start
  298.1 471.1 %collective-permute-start = (f32[3,1,128,128]{3,2,0,1:T(8,128)S(1)}, f32[3,1,128,128]{3,2,0,1:T(8,128)S(1)}, u32[]{:S(2)}, u32[]{:S(2)}) collective-permute-start(f32[3,1,128,128]{3,2,0,1:T(8,128)S(1)} %get-tuple-element.889), channel_id=1, source_target_pairs={{0,16},{16,32},{32,48},{48,64},{64,80},{80,96},{96,112},{112,128},... | collective-permute-start | bytes 589832 | tf_op jit(solution)/shard_map/while/body/eval_jaxpr/ppermute | solution.py:18
  905.0 7.6 collective-permute-start.1
  912.6 7.6 collective-permute-start.1
  920.1 7.9 collective-permute-start.1
  928.0 9.1 collective-permute-start.1
  937.1 9.1 collective-permute-start.1
  946.2 8.2 collective-permute-start.1
  954.5 7.6 collective-permute-start.1
  962.0 7.6 collective-permute-start.1
  977.1 8.6 collective-permute-start.1
  985.7 11.1 collective-permute-start.1
  996.8 9.9 collective-permute-start.1
  1006.7 8.7 collective-permute-start.1
  1015.4 9.1 collective-permute-start.1
  1024.5 9.7 collective-permute-start.1
  1034.1 274.6 %collective-permute-start.1 = (f32[3,1,128,128]{3,2,0,1:T(8,128)S(1)}, f32[3,1,128,128]{3,2,0,1:T(8,128)S(1)}, u32[]{:S(2)}, u32[]{:S(2)}) collective-permute-start(f32[3,1,128,128]{3,2,0,1:T(8,128)S(1)} %get-tuple-element.925), channel_id=1, source_target_pairs={{0,16},{16,32},{32,48},{48,64},{64,80},{80,96},{96,112},{112,128},... | collective-permute-start | bytes 589832 | tf_op jit(solution)/shard_map/while/body/eval_jaxpr/ppermute | solution.py:18
  (9 other events, 471.6 us)
where the time goes:
time: 1410 us; the launch traced here: 1390 us
  waiting for transfers between devices  1030 us (73%)
  blocking collectives  209 us (15%)
  matrix products  65.7 us (5%)
  starting transfers between devices  49.5 us (4%)
  local copies, waits for them, and re-layouts  15.9 us (1%)
  loops' own time  15.5 us (1%)
    ppermute x32, waiting for transfers between devices, passed_along(): return lax.ppermute(value, axis, pairs)  991 us
    psum x2, blocking collectives, body(): totals = lax.psum(jnp.sum(widened * widened, axis=1), 'tok')  172 us
    ppermute x32, starting transfers between devices, passed_along(): return lax.ppermute(value, axis, pairs)  41 us
    all_to_all x1, blocking collectives, body(): lax.all_to_all(final_stream, 'tok', split_axis=0, concat_axis=1, tiled=True)  37.3 us
    all_to_all x1, waiting for transfers between devices, body(): lax.all_to_all(tokens, 'tok', split_axis=1, concat_axis=0, tiled=True)  35.7 us
  transfers between devices with their start and end apart: 33, of which 33 were waited for; matrix products, arithmetic and copies ran while one was open for 0% of the time, Pallas kernels for 0%

commit v1 on v0

v1 whole, which is shorter than its diff:
```python
import functools

import jax
import jax.numpy as jnp
from jax import lax
from jax.experimental import pallas as pl
from jax.experimental.pallas import tpu as pltpu
from jax.sharding import PartitionSpec as P

NS_STEPS = 5
MUON_A = 3.4445
MUON_B = -4.775
MUON_C = 2.0315
EPSILON = 1e-06
CODES = 32767.0
LANES = 128
VMEM_LIMIT = 40 * 1024 * 1024

bf16 = jnp.bfloat16
f32 = jnp.float32


def on_chip():
    return pl.BlockSpec(memory_space=pltpu.VMEM)


def params():
    return pltpu.CompilerParams(vmem_limit_bytes=VMEM_LIMIT)


def dot(left, right):
    return jnp.dot(left, right, preferred_element_type=f32)


def two_parts(value):
    high = value.astype(bf16)
    return high, (value - high.astype(f32)).astype(bf16)


def dot_parts(left, right):
    (lh, ll), (rh, rl) = left, right
    width = rh.shape[1]
    weights = jnp.concatenate(
        [jnp.concatenate([rh, rl], axis=1), jnp.concatenate([rh, jnp.zeros_like(rl)], axis=1)], axis=0
    )
    both = dot(jnp.concatenate([lh, ll], axis=1), weights)
    return both[:, :width] + both[:, width:]


def orthogonalize(gradients):
    current = [
        g * lax.rsqrt(jnp.sum(jnp.sum(g * g, axis=1, keepdims=True), axis=0, keepdims=True) + EPSILON)
        for g in gradients
    ]
    for _ in range(NS_STEPS):
        parts = [two_parts(x) for x in current]
        turned = [two_parts(x.T) for x in current]
        square = [dot_parts(p, t) for p, t in zip(parts, turned)]
        halves = [two_parts(s) for s in square]
        polynom = [MUON_B * s + MUON_C * dot_parts(h, h) for s, h in zip(square, halves)]
        current = [
            MUON_A * x + dot_parts(two_parts(q), p) for x, q, p in zip(current, polynom, parts)
        ]
    return current


def moved_on(weights, step, direction, axis):
    moved = weights + step * direction
    before = jnp.sqrt(jnp.sum(weights * weights, axis=axis, keepdims=True) + EPSILON)
    after = jnp.sqrt(jnp.sum(moved * moved, axis=axis, keepdims=True) + EPSILON)
    return moved * (before / after)


def encode(weights, inverse_unit):
    codes = jnp.clip(jnp.round(weights * inverse_unit), -CODES, CODES)
    return codes.astype(jnp.int32).astype(jnp.int16)


def decode(codes, unit):
    return codes.astype(jnp.int32).astype(f32) * unit


def setup_body(slack, init_ref, code_ref, unit_ref, inverse_ref):
    for index in range(init_ref.shape[0]):
        weights = init_ref[index]
        down = index % 3 == 2
        if down:
            weights = weights.T
        total = jnp.sum(weights * weights, axis=1 if down else 0, keepdims=True) + slack
        unit = jnp.broadcast_to(jnp.sqrt(total) * (1.001 / CODES), weights.shape)
        inverse = 1.0 / unit
        unit_ref[index] = unit
        inverse_ref[index] = inverse
        code_ref[index] = encode(weights, inverse)


def setup(fast_init, groups):
    flat = fast_init.reshape((-1,) + fast_init.shape[-2:])
    return pl.pallas_call(
        functools.partial(setup_body, (groups + 2) * EPSILON),
        out_shape=(
            jax.ShapeDtypeStruct(flat.shape, jnp.int16),
            jax.ShapeDtypeStruct(flat.shape, f32),
            jax.ShapeDtypeStruct(flat.shape, f32),
        ),
        in_specs=[on_chip()],
        out_specs=(on_chip(),) * 3,
        compiler_params=params(),
        name="setup",
    )(flat)


def pack_body(x_ref, o_ref):
    rows, width = x_ref.shape
    heads = width // LANES
    total = jnp.zeros((rows, LANES), f32)
    for head in range(heads):
        piece = x_ref[:, head * LANES : (head + 1) * LANES]
        o_ref[head, :rows, :] = piece
        wide = piece.astype(f32)
        total = total + wide * wide
    lines = [
        jnp.sum(total[r * LANES : (r + 1) * LANES].T, axis=0, keepdims=True) for r in range(rows // LANES)
    ]
    inverse = lax.rsqrt(jnp.concatenate(lines, axis=0) / width + EPSILON)
    high = inverse.astype(bf16).astype(f32)
    middle = (inverse - high).astype(bf16).astype(f32)
    low = inverse - high - middle
    tail = jnp.concatenate([high, middle, low, jnp.zeros_like(low)], axis=0).astype(bf16)
    for head in range(heads):
        o_ref[head, rows:, :] = tail


def pack(x):
    rows, width = x.shape
    tail = 4 * (rows // LANES)
    return pl.pallas_call(
        pack_body,
        out_shape=jax.ShapeDtypeStruct((width // LANES, rows + tail, LANES), bf16),
        compiler_params=params(),
        name="pack",
    )(x)


def prep_body(inverse_inside, rows, *refs):
    if inverse_inside:
        x_ref, rate_ref, gain_ref, k_ref, kt_ref, t_ref, tt_ref, inverse_out = refs
    else:
        x_ref, inverse_ref, rate_ref, gain_ref, k_ref, kt_ref, t_ref, tt_ref = refs
    lines = rows // LANES
    norm = jnp.broadcast_to(gain_ref[:, 0:1], (LANES, LANES))
    key = jnp.broadcast_to(gain_ref[:, 2:3], (LANES, LANES))
    value = jnp.broadcast_to(gain_ref[:, 3:4], (LANES, LANES))

    def one(block, carry):
        if inverse_inside:
            tail = x_ref[block, rows:, :].astype(f32)
            inverse = tail[:lines] + tail[lines : 2 * lines] + tail[2 * lines : 3 * lines]
            inverse_out[block] = inverse
        else:
            inverse = inverse_ref[block]
        rate = rate_ref[block]
        for r in range(lines):
            at = pl.multiple_of(block * rows + r * LANES, LANES)
            turned = x_ref[block, r * LANES : (r + 1) * LANES, :].T.astype(f32)
            normed = turned * inverse[r : r + 1] * norm
            keys = (normed * key).astype(bf16)
            values = (normed * value).astype(bf16)
            targets = (rate[r : r + 1] * values.astype(f32)).astype(bf16)
            kt_ref[:, pl.ds(at, LANES)] = keys
            tt_ref[:, pl.ds(at, LANES)] = targets
            k_ref[pl.ds(at, LANES), :] = keys.T
            t_ref[pl.ds(at, LANES), :] = targets.T
        return carry

    lax.fori_loop(0, x_ref.shape[0], one, 0)


def prep(x, inverse, rates, gains, rows):
    blocks = x.shape[0]
    tall = jax.ShapeDtypeStruct((blocks * rows, LANES), bf16)
    flat = jax.ShapeDtypeStruct((LANES, blocks * rows), bf16)
    inside = inverse is None
    shapes = [tall, flat, tall, flat]
    operands = [x, rates, gains] if inside else [x, inverse, rates, gains]
    if inside:
        shapes.append(jax.ShapeDtypeStruct((blocks, rows // LANES, LANES), f32))
    return pl.pallas_call(
        functools.partial(prep_body, inside, rows),
        out_shape=tuple(shapes),
        in_specs=[on_chip()] * len(operands),
        out_specs=(on_chip(),) * len(shapes),
        compiler_params=params(),
        name="prep",
    )(*operands)


def tick_body(chunk, step_ref, w_ref, unit_ref, inverse_ref, k_ref, kt_ref, t_ref, tt_ref, o_ref):
    weights = [decode(w_ref[j], unit_ref[j]) for j in range(3)]
    gate_up = jnp.concatenate([weights[0].astype(bf16), weights[1].astype(bf16)], axis=1)
    down = weights[2].astype(bf16)

    def part(at):
        both = dot(k_ref[at : at + chunk, :], gate_up)
        back = dot(t_ref[at : at + chunk, :], down)
        gate, up = both[:, :LANES], both[:, LANES:]
        sig = 0.5 * jnp.tanh(0.5 * gate) + 0.5
        act = gate * sig
        hidden = (act * up).astype(bf16)
        back_up = (back * act).astype(bf16)
        back_gate = (back * up * (sig + act * (1.0 - sig))).astype(bf16)
        return (
            dot(kt_ref[:, at : at + chunk], jnp.concatenate([back_gate, back_up], axis=1)),
            dot(tt_ref[:, at : at + chunk], hidden),
        )

    first, second = part(0)
    for at in range(chunk, k_ref.shape[0], chunk):
        more_first, more_second = part(at)
        first = first + more_first
        second = second + more_second
    direction = orthogonalize([first[:, :LANES], first[:, LANES:], second])
    for j in range(3):
        fresh = moved_on(weights[j], step_ref[0], direction[j], 1 if j == 2 else 0)
        o_ref[j] = encode(fresh, inverse_ref[j])


def tick(step, codes, unit, inverse_unit, prepared):
    return pl.pallas_call(
        functools.partial(tick_body, min(2048, prepared[0].shape[0])),
        out_shape=jax.ShapeDtypeStruct(codes.shape, jnp.int16),
        in_specs=[pl.BlockSpec(memory_space=pltpu.SMEM)] + [on_chip()] * 7,
        out_specs=on_chip(),
        compiler_params=params(),
        name="tick",
    )(step, codes, unit, inverse_unit, *prepared)


def mix_body(rows, x_ref, inverse_ref, gain_ref, row_ref, w_ref, unit_ref, o_ref, part_ref):
    weights = [decode(w_ref[j], unit_ref[j]).astype(bf16) for j in range(3)]
    gate_up = jnp.concatenate(weights[:2], axis=1)
    down = weights[2].T
    norm = jnp.broadcast_to(gain_ref[:, 0:1], (LANES, LANES))
    query = jnp.broadcast_to(gain_ref[:, 1:2], (LANES, LANES))
    scale = row_ref[4:5, :]
    lines = rows // LANES
    for block in range(x_ref.shape[0]):
        inverse = inverse_ref[block]
        pieces = []
        for r in range(lines):
            turned = x_ref[block, r * LANES : (r + 1) * LANES, :].T.astype(f32)
            pieces.append((turned * inverse[r : r + 1] * norm * query).astype(bf16).T)
        both = dot(jnp.concatenate(pieces, axis=0), gate_up)
        gate, up = both[:, :LANES], both[:, LANES:]
        hidden = (gate * (0.5 * jnp.tanh(0.5 * gate) + 0.5) * up).astype(bf16)
        output = dot(hidden, down)
        mixed = (x_ref[block, :rows, :].astype(f32) + scale * output).astype(bf16)
        o_ref[block] = mixed
        wide = mixed.astype(f32)
        wide = wide * wide
        part_ref[block] = jnp.concatenate(
            [jnp.sum(wide[r * LANES : (r + 1) * LANES].T, axis=0, keepdims=True) for r in range(lines)], axis=0
        )


def mix(x, inverse, gains, gain_rows, codes, unit, rows):
    blocks = x.shape[0]
    step = 4
    lines = rows // LANES
    whole = lambda i: (0, 0)
    cube = lambda i: (0, 0, 0)
    moving = lambda i: (i, 0, 0)
    return pl.pallas_call(
        functools.partial(mix_body, rows),
        out_shape=(
            jax.ShapeDtypeStruct((blocks, rows, LANES), bf16),
            jax.ShapeDtypeStruct((blocks, lines, LANES), f32),
        ),
        grid=(blocks // step,),
        in_specs=[
            pl.BlockSpec((step, rows, LANES), moving),
            pl.BlockSpec((step, lines, LANES), moving),
            pl.BlockSpec(gains.shape, whole),
            pl.BlockSpec(gain_rows.shape, whole),
            pl.BlockSpec(codes.shape, cube),
            pl.BlockSpec(unit.shape, cube),
        ],
        out_specs=(
            pl.BlockSpec((step, rows, LANES), moving),
            pl.BlockSpec((step, lines, LANES), moving),
        ),
        compiler_params=params(),
        name="mix",
    )(x, inverse, gains, gain_rows, codes, unit)


def unpack_body(x_ref, o_ref):
    for head in range(x_ref.shape[0]):
        o_ref[:, head * LANES : (head + 1) * LANES] = x_ref[head]


def unpack(x):
    heads, rows, lanes = x.shape
    step = min(rows, 128)
    return pl.pallas_call(
        unpack_body,
        out_shape=jax.ShapeDtypeStruct((rows, heads * lanes), x.dtype),
        grid=(rows // step,),
        in_specs=[pl.BlockSpec((heads, step, lanes), lambda i: (0, i, 0))],
        out_specs=pl.BlockSpec((step, heads * lanes), lambda i: (i, 0)),
        compiler_params=params(),
        name="unpack",
    )(x)


def passed_on(value, index, groups):
    def hop(source):
        return lambda sent: lax.ppermute(sent, "group", [(source, source + 1)])

    return lax.switch(index, [hop(source) for source in range(groups - 1)], value)


def body(tokens, learning_rates, channel_gains, fast_init, step_size, update_table):
    groups = lax.axis_size("group")
    ranks = lax.axis_size("tok")
    me = lax.axis_index("group")
    rows, width = tokens.shape
    layers = fast_init.shape[0]
    lines = rows // LANES

    codes, unit, inverse_unit = setup(fast_init, groups)
    columns = jnp.swapaxes(channel_gains, 1, 2)
    rates = learning_rates.reshape(layers, ranks, lines, LANES)
    stream = lax.all_to_all(pack(tokens), "tok", split_axis=0, concat_axis=0, tiled=True)
    inverse = None

    for layer in range(layers):
        chosen = slice(3 * layer, 3 * layer + 3)
        prepared = prep(stream, inverse, rates[layer], columns[layer], rows)
        if inverse is None:
            inverse = prepared[4]
        prepared = prepared[:4]
        flag = lax.dynamic_index_in_dim(update_table[layer], me, 0, keepdims=False) != 0
        step = step_size[layer]
        layer_unit, layer_inverse = unit[chosen], inverse_unit[chosen]

        def one(index, entering):
            leaving = lax.cond(
                (index == me) & flag,
                lambda held: tick(step, held, layer_unit, layer_inverse, prepared),
                lambda held: held,
                entering,
            )
            received = passed_on(leaving, index, groups)
            return jnp.where(index == me - 1, received, entering)

        entering = lax.fori_loop(
            jnp.maximum(me - 1, 0), jnp.minimum(me + 1, groups - 1), one, codes[chosen]
        )
        stream, partial = mix(
            stream, inverse, columns[layer], channel_gains[layer], entering, layer_unit, rows
        )
        if layer + 1 < layers:
            mine = jnp.sum(lax.all_to_all(partial, "tok", 0, 0, tiled=True), axis=0)
            mine = lax.rsqrt(mine / width + EPSILON)
            inverse = lax.all_to_all(
                jnp.broadcast_to(mine[None], (ranks, lines, LANES)), "tok", 0, 0, tiled=True
            )
    return unpack(lax.all_to_all(stream, "tok", split_axis=0, concat_axis=0, tiled=True))


def solution(mesh):
    in_specs = (
        P(("group", "tok"), None),
        P(None, "group"),
        P(None, None, "tok"),
        P(None, None, "tok", None, None),
        P(None, "tok"),
        P(),
    )
    out_specs = P(("group", "tok"), None)
    return jax.shard_map(body, mesh=mesh, in_specs=in_specs, out_specs=out_specs, check_vma=False)
```

time: 1410 us -> 391 us (0.28); the launches traced: 1390 us -> 394 us
  waiting for transfers between devices: 1030 us -> 285 us
  blocking collectives: 209 us -> 47.8 us
  matrix products: 65.7 us -> 0 us
  starting transfers between devices: 49.5 us -> 14.5 us
  Pallas kernels: 0 us -> 29.6 us
    ppermute x32 -> x2, waiting for transfers between devices: 991 us -> 244 us  [hop(): return lambda sent: lax.ppermute(sent, 'group', [(source, source + 1)])]
    psum x2 -> x0, blocking collectives: 172 us -> none  [body(): totals = lax.psum(jnp.sum(widened * widened, axis=1), 'tok')]
    dot_general x46 -> x0, matrix products: 65.7 us -> none  [the longest x2 14.3 us: layer_group(): jnp.einsum('thj,hjk->thk', hidden_q, rounded[2], preferred_element_type=j...]
    ppermute x32 -> x2, starting transfers between devices: 41 us -> 2.58 us  [hop(): return lambda sent: lax.ppermute(sent, 'group', [(source, source + 1)])]
    pallas_call x0 -> x7, Pallas kernels: none -> 29.6 us  [the longest x2 13.8 us: prep(): pl.pallas_call(functools.partial(prep_body, inside, rows), out_shape=tupl...]
    all_to_all x1 -> x2, blocking collectives: 37.3 us -> 47.8 us  [the longest x1 34.2 us: body(): lax.all_to_all(stream, 'tok', split_axis=0, concat_axis=0, tiled=True)]
    all_to_all x1 -> x2, waiting for transfers between devices: 35.7 us -> 41.5 us  [the longest x1 32.1 us: body(): lax.all_to_all(pack(tokens), 'tok', split_axis=0, concat_axis=0, tiled=True)]
  transfers between devices with their start and end apart: 33 -> 4, of which waited for: 33 -> 4; matrix products, arithmetic and copies ran while one was open for 0% -> 2% of each run, Pallas kernels for 0% -> 0%
where the time goes in v1:
time: 391 us; the launch traced here: 394 us
  waiting for transfers between devices  285 us (73%)
  blocking collectives  47.8 us (12%)
  Pallas kernels  29.6 us (8%)
  starting transfers between devices  14.5 us (4%)
  local copies, waits for them, and re-layouts  11.9 us (3%)
    ppermute x2, waiting for transfers between devices, hop(): return lambda sent: lax.ppermute(sent, 'group', [(source, source + 1)])  244 us
    all_to_all x1, blocking collectives, body(): lax.all_to_all(stream, 'tok', split_axis=0, concat_axis=0, tiled=True)  34.2 us
    all_to_all x1, waiting for transfers between devices, body(): lax.all_to_all(pack(tokens), 'tok', split_axis=0, concat_axis=0, tiled=True)  32.1 us
    pallas_call x2, Pallas kernels, prep(): pl.pallas_call(functools.partial(prep_body, inside, rows), out_shape=tupl...  13.8 us
    all_to_all x1, blocking collectives, body(): mine = jnp.sum(lax.all_to_all(partial, 'tok', 0, 0, tiled=True), axis=0)  13.5 us
    pallas_call x2, Pallas kernels, mix(): pl.pallas_call(functools.partial(mix_body, rows), out_shape=(jax.ShapeDty...  12.6 us
    all_to_all x1, waiting for transfers between devices, body(): lax.all_to_all(jnp.broadcast_to(mine[None], (ranks, lines, LANES)), 'tok'...  9.38 us
    all_to_all x1, starting transfers between devices, body(): lax.all_to_all(pack(tokens), 'tok', split_axis=0, concat_axis=0, tiled=True)  8.48 us
  transfers between devices with their start and end apart: 4, of which 4 were waited for; matrix products, arithmetic and copies ran while one was open for 2% of the time, Pallas kernels for 0%

profile of v1, /device:TPU:120, one launch (start us, length us, event | category | flops | bytes accessed | tf_op | source)
XLA Modules:
  0.0 394.0 jit_solution(13096723698844746525)
XLA Ops:
  0.0 1.6 copy-done.4
  1.6 0.7 pack.1
  2.3 1.4 copy-done
  3.6 8.5 %all-to-all-start = ((bf16[16,528,128]{2,1,0:T(8,128)(2,1)}), bf16[16,528,128]{2,1,0:T(8,128)(2,1)S(1)}, u32[]{:S(2)}, u32[]{:S(2)}) async-start(bf16[16,528,128]{2,1,0:T(8,128)(2,1)} %copy-done), calls=%async_computation | async-start | bytes 4325376 | tf_op jit(solution)/shard_map/all_to_all | solution.py:334
  12.1 0.8 copy.7
  14.3 0.6 fusion.6
  15.0 0.9 slice_bitcast_fusion
  15.8 0.6 fusion.2
  16.5 0.9 fusion
  17.4 1.0 fusion.3
  18.4 32.1 %all-to-all-done.refs_0_.x_ref = bf16[16,528,128]{2,1,0:T(8,128)(2,1)S(1)} async-done(((bf16[16,528,128]{2,1,0:T(8,128)(2,1)}), bf16[16,528,128]{2,1,0:T(8,128)(2,1)S(1)}, u32[]{:S(2)}, u32[]{:S(2)}) %all-to-all-start) | async-done | bytes 2162720 | tf_op jit(solution)/shard_map/all_to_all | solution.py:334
  50.5 7.0 %prep.2 = (bf16[8192,128]{1,0:T(8,128)(2,1)}, bf16[128,8192]{1,0:T(8,128)(2,1)}, bf16[8192,128]{1,0:T(8,128)(2,1)}, bf16[128,8192]{1,0:T(8,128)(2,1)}, f32[16,4,128]{2,1,0:T(4,128)S(1)}) custom-call(bf16[16,528,128]{2,1,0:T(8,128)(2,1)S(1)} %all-to-all-done.refs_0_.x_ref, f32[16,4,128]{2,1,0:T(4,128)S(1)} %bitcast.20, ...), custom_call_target="tpu_custom_call" | custom-call | tf_op jit(solution)/shard_map/prep/pallas_call | solution.py:188
  57.5 226.6 %while.30 = (s32[]{:T(128)}, s16[3,128,128]{2,1,0:T(8,128)(2,1)S(1)}, s32[]{:T(128)}, s32[]{:T(128)}, s32[]{:T(128)}, /*index=5*/pred[]{:T(512)}, f32[1]{0:T(128...) while((s32[]{:T(128)}, ...), condition=%wide.region_18.19_spmd, body=%wide.region_0.18_spmd.sunk | while | flops 49159 | bytes 885056 | solution.py:357
  58.1 225.0 %conditional.9 = (s16[3,128,128]{2,1,0:T(8,128)(2,1)}) conditional(s32[]{:T(128)} %clamp.12, s16[3,128,128]{2,1,0:T(8,128)(2,1)S(1)} %get-tuple-element.777, s16[3,128,128]{2,1,0:T(8,128)(2,1)S(1)} %get-tuple-element.777, s16[3,128,128]{2,1,0:T(8,128)(2,1)S(1)} %get-tuple-element.777, ...), branch_computations={%region_3.3_spmd, %region_4.4_spmd, %region_5.5_spmd, %region_6.6_... | conditional | bytes 393264 | solution.py:320
  58.1 1.3 collective-permute-start.14
  59.4 223.7 %collective-permute-done.14 = s16[3,128,128]{2,1,0:T(8,128)(2,1)} collective-permute-done((s16[3,128,128]{2,1,0:T(8,128)(2,1)S(1)}, s16[3,128,128]{2,1,0:T(8,128)(2,1)}, u32[]{:S(2)}, u32[]{:S(2)}) %collective-permute-start.14) | collective-permute-done | bytes 98336 | tf_op jit(solution)/shard_map/while/body/cond/branch_14_fun/ppermute | solution.py:318
  283.1 1.0 broadcast_select_fusion.4
  284.1 6.1 %mix.2 = (bf16[16,512,128]{2,1,0:T(8,128)(2,1)S(1)}, f32[16,4,128]{2,1,0:T(4,128)S(1)}) custom-call(bf16[16,528,128]{2,1,0:T(8,128)(2,1)S(1)} %all-to-all-done.refs_0_.x_ref, f32[16,4,128]{2,1,0:T(4,128)S(1)} %get-tuple-element.434.inverse_ref, f32[128,5]{1,0:T(8,128)S(1)} %get-tuple-element.510.refs_2_.gain_ref, f32[5,128]{1,0:T(8,128)S(1)} %bitcast.21, ...), custom_call_target="tpu_custom_call" | custom-call | tf_op jit(solution)/shard_map/mix/pallas_call | solution.py:273
  290.2 1.3 copy-done.1
  291.5 13.5 %all_to_all.20 = f32[16,4,128]{2,1,0:T(4,128)S(1)} all-to-all(f32[16,4,128]{2,1,0:T(4,128)S(1)} %get-tuple-element.444), channel_id=1, replica_groups=mesh['group'=16,'tok'=16] {'tok'}, dimensions={0} | all-to-all | bytes 65536 | tf_op jit(solution)/shard_map/all_to_all | solution.py:364
  305.8 3.5 all-to-all-start.2
  309.8 9.4 %all-to-all-done.2.refs_1_.inverse_ref = f32[16,4,128]{2,1,0:T(4,128)S(1)} async-done(((f32[16,4,128]{2,1,0:T(4,128)}), f32[16,4,128]{2,1,0:T(4,128)S(1)}, u32[]{:S(2)}, u32[]{:S(2)}) %all-to-all-start.2) | async-done | bytes 32800 | tf_op jit(solution)/shard_map/all_to_all | solution.py:366
  319.2 1.6 copy-done.2
  320.8 6.9 %prep.3 = (bf16[8192,128]{1,0:T(8,128)(2,1)}, bf16[128,8192]{1,0:T(8,128)(2,1)}, bf16[8192,128]{1,0:T(8,128)(2,1)}, bf16[128,8192]{1,0:T(8,128)(2,1)}) custom-call(bf16[16,512,128]{2,1,0:T(8,128)(2,1)S(1)} %copy-done.2, f32[16,4,128]{2,1,0:T(4,128)S(1)} %all-to-all-done.2.refs_1_.inverse_ref, f32[16,4,128]{2,1,0:T(4,128)S(1)} %bitcast.19, ...), custom_call_target="tpu_custom_call" | custom-call | tf_op jit(solution)/shard_map/prep/pallas_call | solution.py:188
  327.7 23.3 %while.31 = (s32[]{:T(128)}, s16[3,128,128]{2,1,0:T(8,128)(2,1)S(1)}, s32[]{:T(128)}, s32[]{:T(128)}, s32[]{:T(128)}, /*index=5*/pred[]{:T(512)}, f32[1]{0:T(128...) while((s32[]{:T(128)}, ...), condition=%wide.region_38.39_spmd, body=%wide.region_20.38_spmd.sunk | while | flops 49159 | bytes 885056 | solution.py:357
  328.6 21.5 %conditional.11 = (s16[3,128,128]{2,1,0:T(8,128)(2,1)}) conditional(s32[]{:T(128)} %clamp.13, s16[3,128,128]{2,1,0:T(8,128)(2,1)S(1)} %get-tuple-element.779, s16[3,128,128]{2,1,0:T(8,128)(2,1)S(1)} %get-tuple-element.779, s16[3,128,128]{2,1,0:T(8,128)(2,1)S(1)} %get-tuple-element.779, ...), branch_computations={%region_23.23_spmd, %region_24.24_spmd, %region_25.25_spmd, %regio... | conditional | bytes 393264 | solution.py:320
  328.6 1.3 collective-permute-start.29
  329.9 20.2 %collective-permute-done.29 = s16[3,128,128]{2,1,0:T(8,128)(2,1)} collective-permute-done((s16[3,128,128]{2,1,0:T(8,128)(2,1)S(1)}, s16[3,128,128]{2,1,0:T(8,128)(2,1)}, u32[]{:S(2)}, u32[]{:S(2)}) %collective-permute-start.29) | collective-permute-done | bytes 98336 | tf_op jit(solution)/shard_map/while/body/cond/branch_14_fun/ppermute | solution.py:318
  350.1 1.0 broadcast_select_fusion.5
  351.1 6.5 %mix.3 = (bf16[16,512,128]{2,1,0:T(8,128)(2,1)S(1)}, f32[16,4,128]{2,1,0:T(4,128)}) custom-call(bf16[16,512,128]{2,1,0:T(8,128)(2,1)S(1)} %copy-done.3, f32[16,4,128]{2,1,0:T(4,128)S(1)} %all-to-all-done.2.refs_1_.inverse_ref, f32[128,5]{1,0:T(8,128)S(1)} %get-tuple-element.509.refs_3_.gain_ref, f32[5,128]{1,0:T(8,128)S(1)} %bitcast.22, ...), custom_call_target="tpu_custom_call" | custom-call | tf_op jit(solution)/shard_map/mix/pallas_call | solution.py:273
  357.6 34.2 %all_to_all.21.x_ref = bf16[16,512,128]{2,1,0:T(8,128)(2,1)S(1)} all-to-all(bf16[16,512,128]{2,1,0:T(8,128)(2,1)S(1)} %get-tuple-element.450), channel_id=1, replica_groups=mesh['group'=16,'tok'=16] {'tok'}, dimensions={0} | all-to-all | bytes 4194304 | tf_op jit(solution)/shard_map/all_to_all | solution.py:369
  391.8 2.1 unpack.1
  (40 shorter events, 2.7 us)
Async XLA Ops:
  0.0 1.6 copy-start.4
  2.2 1.4 copy-start
  3.6 8.5 %copy-start.11 = (f32[2,5,128]{2,0,1:T(2,128)S(1)}, f32[2,5,128]{2,0,1:T(2,128)}, u32[]{:S(2)}) copy-start(f32[2,5,128]{2,0,1:T(2,128)} %param.46) | copy-start | bytes 15364
  3.6 9.3 %copy-start.5 = (f32[2,3,1,128,128]{4,3,2,1,0:T(8,128)S(1)}, f32[2,3,1,128,128]{4,3,2,1,0:T(8,128)}, u32[]{:S(2)}) copy-start(f32[2,3,1,128,128]{4,3,2,1,0:T(8,128)} %param.47) | copy-start | bytes 1179652
  3.6 9.6 %copy-start.13 = (s32[2,16]{1,0:T(2,128)S(1)}, s32[2,16]{1,0:T(2,128)}, u32[]{:S(2)}) copy-start(s32[2,16]{1,0:T(2,128)} %param.49) | copy-start | bytes 388
  3.6 10.7 %copy-start.12 = (f32[2,1]{0,1:T(1,128)S(1)}, f32[2,1]{0,1:T(1,128)}, u32[]{:S(2)}) copy-start(f32[2,1]{0,1:T(1,128)} %param.48) | copy-start | bytes 28
  3.6 46.9 %all-to-all-start = ((bf16[16,528,128]{2,1,0:T(8,128)(2,1)}), bf16[16,528,128]{2,1,0:T(8,128)(2,1)S(1)}, u32[]{:S(2)}, u32[]{:S(2)}) async-start(bf16[16,528,128]{2,1,0:T(8,128)(2,1)} %copy-done), calls=%async_computation | async-start | bytes 4325376 | tf_op jit(solution)/shard_map/all_to_all | solution.py:334
  16.5 41.0 %copy-start.6 = (s16[3,128,128]{2,1,0:T(8,128)(2,1)S(1)}, s16[3,128,128]{2,1,0:T(8,128)(2,1)}, u32[]{:S(2)}) copy-start(s16[3,128,128]{2,1,0:T(8,128)(2,1)} %get-tuple-element.682) | copy-start | bytes 294916
  17.4 40.1 %copy-start.8 = (f32[3,128,128]{2,1,0:T(8,128)S(1)}, f32[3,128,128]{2,1,0:T(8,128)}, u32[]{:S(2)}) copy-start(f32[3,128,128]{2,1,0:T(8,128)} %get-tuple-element.688.unit_ref) | copy-start | bytes 589828
  17.4 40.1 %copy-start.10 = (f32[3,128,128]{2,1,0:T(8,128)S(1)}, f32[3,128,128]{2,1,0:T(8,128)}, u32[]{:S(2)}) copy-start(f32[3,128,128]{2,1,0:T(8,128)} %get-tuple-element.689) | copy-start | bytes 589828
  58.1 225.0 %collective-permute-start.14 = (s16[3,128,128]{2,1,0:T(8,128)(2,1)S(1)}, s16[3,128,128]{2,1,0:T(8,128)(2,1)}, u32[]{:S(2)}, u32[]{:S(2)}) collective-permute-start(s16[3,128,128]{2,1,0:T(8,128)(2,1)S(1)} %param.16), channel_id=1, source_target_pairs={{224,240},{225,241},{226,242},{227,243},{228,244},{229,245},{230,2... | collective-permute-start | bytes 294920 | tf_op jit(solution)/shard_map/while/body/cond/branch_14_fun/ppermute | solution.py:318
  284.1 25.2 %copy-start.14 = (s32[1,16]{1,0:T(1,128)S(1)}, s32[1,16]{1,0:T(1,128)}, u32[]{:S(2)}) copy-start(s32[1,16]{1,0:T(1,128)} %get-tuple-element.515) | copy-start | bytes 196
  284.1 43.6 %copy-start.7 = (f32[3,128,128]{2,1,0:T(8,128)S(1)}, f32[3,128,128]{2,1,0:T(8,128)}, u32[]{:S(2)}) copy-start(f32[3,128,128]{2,1,0:T(8,128)} %get-tuple-element.736.unit_ref) | copy-start | bytes 589828
  284.1 43.6 %copy-start.9 = (f32[3,128,128]{2,1,0:T(8,128)S(1)}, f32[3,128,128]{2,1,0:T(8,128)}, u32[]{:S(2)}) copy-start(f32[3,128,128]{2,1,0:T(8,128)} %get-tuple-element.737) | copy-start | bytes 589828
  290.2 1.3 copy-start.1
  305.8 13.4 %all-to-all-start.2 = ((f32[16,4,128]{2,1,0:T(4,128)}), f32[16,4,128]{2,1,0:T(4,128)S(1)}, u32[]{:S(2)}, u32[]{:S(2)}) async-start(f32[16,4,128]{2,1,0:T(4,128)} %broadcast_in_dim.2), calls=%async_computation.2 | async-start | bytes 65536 | tf_op jit(solution)/shard_map/all_to_all | solution.py:366
  319.2 1.6 copy-start.2
  327.7 23.4 %copy-start.3 = (bf16[16,512,128]{2,1,0:T(8,128)(2,1)S(1)}, bf16[16,512,128]{2,1,0:T(8,128)(2,1)}, u32[]{:S(2)}) copy-start(bf16[16,512,128]{2,1,0:T(8,128)(2,1)} %copy-done.1) | copy-start | bytes 6291460
  328.6 21.5 %collective-permute-start.29 = (s16[3,128,128]{2,1,0:T(8,128)(2,1)S(1)}, s16[3,128,128]{2,1,0:T(8,128)(2,1)}, u32[]{:S(2)}, u32[]{:S(2)}) collective-permute-start(s16[3,128,128]{2,1,0:T(8,128)(2,1)S(1)} %param.35), channel_id=1, source_target_pairs={{224,240},{225,241},{226,242},{227,243},{228,244},{229,245},{230,2... | collective-permute-start | bytes 294920 | tf_op jit(solution)/shard_map/while/body/cond/branch_14_fun/ppermute | solution.py:318

commit v2 on v1

v2 whole, which is shorter than its diff:
```python
import functools

import jax
import jax.numpy as jnp
from jax import lax
from jax.experimental import pallas as pl
from jax.experimental.pallas import tpu as pltpu
from jax.sharding import PartitionSpec as P

NS_STEPS = 5
MUON_A = 3.4445
MUON_B = -4.775
MUON_C = 2.0315
EPSILON = 1e-06
CODES = 32767.0
LANES = 128

bf16 = jnp.bfloat16
f32 = jnp.float32


def on_chip():
    return pl.BlockSpec(memory_space=pltpu.VMEM)


def params(mebibytes):
    return pltpu.CompilerParams(vmem_limit_bytes=mebibytes * 1024 * 1024)


def dot(left, right):
    return jnp.dot(left, right, preferred_element_type=f32)


def two_parts(value):
    high = value.astype(bf16)
    return high, (value - high.astype(f32)).astype(bf16)


def dot_parts(left, right):
    (lh, ll), (rh, rl) = left, right
    width = rh.shape[1]
    weights = jnp.concatenate(
        [jnp.concatenate([rh, rl], axis=1), jnp.concatenate([rh, jnp.zeros_like(rl)], axis=1)], axis=0
    )
    both = dot(jnp.concatenate([lh, ll], axis=1), weights)
    return both[:, :width] + both[:, width:]


def orthogonalize(gradients):
    current = [
        g * lax.rsqrt(jnp.sum(jnp.sum(g * g, axis=1, keepdims=True), axis=0, keepdims=True) + EPSILON)
        for g in gradients
    ]
    for _ in range(NS_STEPS):
        parts = [two_parts(x) for x in current]
        turned = [two_parts(x.T) for x in current]
        square = [dot_parts(p, t) for p, t in zip(parts, turned)]
        halves = [two_parts(s) for s in square]
        polynom = [MUON_B * s + MUON_C * dot_parts(h, h) for s, h in zip(square, halves)]
        current = [
            MUON_A * x + dot_parts(two_parts(q), p) for x, q, p in zip(current, polynom, parts)
        ]
    return current


def moved_on(weights, step, direction, axis):
    moved = weights + step * direction
    before = jnp.sqrt(jnp.sum(weights * weights, axis=axis, keepdims=True) + EPSILON)
    after = jnp.sqrt(jnp.sum(moved * moved, axis=axis, keepdims=True) + EPSILON)
    return moved * (before / after)


def encode(weights, inverse_unit):
    codes = jnp.clip(jnp.round(weights * inverse_unit), -CODES, CODES)
    return codes.astype(jnp.int32).astype(jnp.int16)


def decode(codes, unit):
    return codes.astype(jnp.int32).astype(f32) * unit


def setup_body(slack, init_ref, code_ref, unit_ref, inverse_ref):
    for index in range(init_ref.shape[0]):
        weights = init_ref[index]
        down = index % 3 == 2
        if down:
            weights = weights.T
        total = jnp.sum(weights * weights, axis=1 if down else 0, keepdims=True) + slack
        unit = jnp.broadcast_to(jnp.sqrt(total) * (1.001 / CODES), weights.shape)
        inverse = 1.0 / unit
        unit_ref[index] = unit
        inverse_ref[index] = inverse
        code_ref[index] = encode(weights, inverse)


def setup(fast_init, groups):
    flat = fast_init.reshape((-1,) + fast_init.shape[-2:])
    return pl.pallas_call(
        functools.partial(setup_body, (groups + 2) * EPSILON),
        out_shape=(
            jax.ShapeDtypeStruct(flat.shape, jnp.int16),
            jax.ShapeDtypeStruct(flat.shape, f32),
            jax.ShapeDtypeStruct(flat.shape, f32),
        ),
        in_specs=[on_chip()],
        out_specs=(on_chip(),) * 3,
        compiler_params=params(20),
        name="setup",
    )(flat)


def pack_body(x_ref, o_ref):
    rows, width = x_ref.shape
    heads = width // LANES
    total = jnp.zeros((rows, LANES), f32)
    for head in range(heads):
        piece = x_ref[:, head * LANES : (head + 1) * LANES]
        o_ref[head, :rows, :] = piece
        wide = piece.astype(f32)
        total = total + wide * wide
    lines = [
        jnp.sum(total[r * LANES : (r + 1) * LANES].T, axis=0, keepdims=True) for r in range(rows // LANES)
    ]
    inverse = lax.rsqrt(jnp.concatenate(lines, axis=0) / width + EPSILON)
    high = inverse.astype(bf16).astype(f32)
    middle = (inverse - high).astype(bf16).astype(f32)
    low = inverse - high - middle
    tail = jnp.concatenate([high, middle, low, jnp.zeros_like(low)], axis=0).astype(bf16)
    for head in range(heads):
        o_ref[head, rows:, :] = tail


def pack(x):
    rows, width = x.shape
    tail = 4 * (rows // LANES)
    return pl.pallas_call(
        pack_body,
        out_shape=jax.ShapeDtypeStruct((width // LANES, rows + tail, LANES), bf16),
        compiler_params=params(20),
        name="pack",
    )(x)


def column_of(lines):
    count = lines.shape[0]
    return jnp.concatenate([lines] * (8 // count), axis=0).T


def prep_body(inverse_inside, rows, *refs):
    if inverse_inside:
        x_ref, rate_ref, gain_ref, early_ref, late_ref, inverse_out = refs
    else:
        x_ref, inverse_ref, rate_ref, gain_ref, early_ref, late_ref = refs
    lines = rows // LANES
    norm, key, value = gain_ref[0:1, :], gain_ref[2:3, :], gain_ref[3:4, :]

    def fill(o_ref):
        for block in range(x_ref.shape[0]):
            if inverse_inside:
                tail = x_ref[block, rows:, :].astype(f32)
                inverse = tail[:lines] + tail[lines : 2 * lines] + tail[2 * lines : 3 * lines]
                inverse_out[block] = inverse
            else:
                inverse = inverse_ref[block]
            inverse = column_of(inverse)
            rate = column_of(rate_ref[block])
            for r in range(lines):
                at = block * rows + r * LANES
                wide = x_ref[block, r * LANES : (r + 1) * LANES, :].astype(f32)
                normed = wide * inverse[:, r : r + 1] * norm
                o_ref[0, at : at + LANES, :] = (normed * key).astype(bf16)
                values = (normed * value).astype(bf16)
                o_ref[1, at : at + LANES, :] = (rate[:, r : r + 1] * values.astype(f32)).astype(bf16)

    half = pl.num_programs(0) // 2

    @pl.when(pl.program_id(0) < half)
    def _():
        fill(early_ref)

    @pl.when(pl.program_id(0) >= half)
    def _():
        fill(late_ref)


def prep(x, inverse, rates, gains, rows):
    blocks, height = x.shape[:2]
    lines = rows // LANES
    step = 4
    half = blocks // step // 2
    pair = jax.ShapeDtypeStruct((2, blocks * rows // 2, LANES), bf16)
    line_spec = pl.BlockSpec((step, lines, LANES), lambda i: (i, 0, 0))
    inside = inverse is None
    shapes = [pair, pair]
    out_specs = [
        pl.BlockSpec((2, step * rows, LANES), lambda i: (0, jnp.minimum(i, half - 1), 0)),
        pl.BlockSpec((2, step * rows, LANES), lambda i: (0, jnp.maximum(i - half, 0), 0)),
    ]
    operands = [x, rates, gains] if inside else [x, inverse, rates, gains]
    in_specs = [pl.BlockSpec((step, height, LANES), lambda i: (i, 0, 0))]
    in_specs += [line_spec] * (len(operands) - 2) + [pl.BlockSpec(gains.shape, lambda i: (0, 0))]
    if inside:
        shapes.append(jax.ShapeDtypeStruct((blocks, lines, LANES), f32))
        out_specs.append(line_spec)
    return pl.pallas_call(
        functools.partial(prep_body, inside, rows),
        out_shape=tuple(shapes),
        grid=(blocks // step,),
        in_specs=in_specs,
        out_specs=tuple(out_specs),
        compiler_params=params(20),
        name="prep",
    )(*operands)


def tick_body(chunk, flag_ref, step_ref, w_ref, unit_ref, inverse_ref, early_ref, late_far, o_ref, kept_ref, late_ref, late_sem):
    updates = flag_ref[0] != 0
    late_in = pltpu.make_async_copy(late_far, late_ref, late_sem)

    @pl.when(updates)
    def _():
        late_in.start()

    kept_ref[...] = w_ref[...]

    @pl.when(jnp.logical_not(updates))
    def _():
        o_ref[...] = w_ref[...]

    @pl.when(updates)
    def _():
        weights = [decode(w_ref[j], unit_ref[j]) for j in range(3)]
        gate_up = jnp.concatenate([weights[0].astype(bf16), weights[1].astype(bf16)], axis=1)
        down = weights[2].astype(bf16)
        over_tokens = functools.partial(
            lax.dot_general, dimension_numbers=(((0,), (0,)), ((), ())), preferred_element_type=f32
        )

        def part(d_ref, at):
            keys = d_ref[0, at : at + chunk, :]
            targets = d_ref[1, at : at + chunk, :]
            both = dot(keys, gate_up)
            back = dot(targets, down)
            gate, up = both[:, :LANES], both[:, LANES:]
            sig = 0.5 * jnp.tanh(0.5 * gate) + 0.5
            act = gate * sig
            hidden = (act * up).astype(bf16)
            back_up = (back * act).astype(bf16)
            back_gate = (back * up * (sig + act * (1.0 - sig))).astype(bf16)
            return (
                over_tokens(keys, jnp.concatenate([back_gate, back_up], axis=1)),
                over_tokens(targets, hidden),
            )

        first, second = part(early_ref, 0)
        for d_ref, begin in ((early_ref, chunk), (late_ref, 0)):
            if d_ref is late_ref:
                late_in.wait()
            for at in range(begin, d_ref.shape[1], chunk):
                more_first, more_second = part(d_ref, at)
                first = first + more_first
                second = second + more_second
        direction = orthogonalize([first[:, :LANES], first[:, LANES:], second])
        for j in range(3):
            fresh = moved_on(weights[j], step_ref[0], direction[j], 1 if j == 2 else 0)
            o_ref[j] = encode(fresh, inverse_ref[j])


def tick(flag, step, codes, unit, inverse_unit, early, late):
    far = pl.BlockSpec(memory_space=pltpu.HBM)
    scalar = pl.BlockSpec(memory_space=pltpu.SMEM)
    shape = jax.ShapeDtypeStruct(codes.shape, jnp.int16)
    return pl.pallas_call(
        functools.partial(tick_body, min(2048, early.shape[1])),
        out_shape=(shape, shape),
        in_specs=[scalar, scalar, on_chip(), on_chip(), on_chip(), on_chip(), far],
        out_specs=(on_chip(), on_chip()),
        scratch_shapes=[
            pltpu.VMEM(late.shape, bf16),
            pltpu.SemaphoreType.DMA,
        ],
        compiler_params=params(24),
        name="tick",
    )(flag, step, codes, unit, inverse_unit, early, late)


def mix_body(rows, x_ref, inverse_ref, gain_ref, w_ref, unit_ref, o_ref, *part_ref):
    weights = [decode(w_ref[j], unit_ref[j]).astype(bf16) for j in range(3)]
    gate_up = jnp.concatenate(weights[:2], axis=1)
    down = weights[2].T
    norm, query, scale = gain_ref[0:1, :], gain_ref[1:2, :], gain_ref[4:5, :]
    lines = rows // LANES
    ones = jnp.ones((8, LANES), bf16)
    for block in range(x_ref.shape[0]):
        inverse = column_of(inverse_ref[block])
        wide = x_ref[block].astype(f32)
        pieces = [
            (wide[r * LANES : (r + 1) * LANES] * inverse[:, r : r + 1] * norm * query).astype(bf16)
            for r in range(lines)
        ]
        both = dot(jnp.concatenate(pieces, axis=0), gate_up)
        gate, up = both[:, :LANES], both[:, LANES:]
        hidden = (gate * (0.5 * jnp.tanh(0.5 * gate) + 0.5) * up).astype(bf16)
        output = dot(hidden, down)
        mixed = (wide + scale * output).astype(bf16)
        o_ref[block] = mixed
        if part_ref:
            square = mixed.astype(f32)
            high, low = two_parts(square * square)
            turned = (((1,), (1,)), ((), ()))
            total = lax.dot_general(ones, high, turned, preferred_element_type=f32) + lax.dot_general(
                ones, low, turned, preferred_element_type=f32
            )
            part_ref[0][block] = jnp.concatenate(
                [total[0:1, r * LANES : (r + 1) * LANES] for r in range(lines)], axis=0
            )


def mix(x, inverse, gains, codes, unit, rows, sums):
    blocks = x.shape[0]
    step = 4
    lines = rows // LANES
    whole = lambda i: (0, 0)
    cube = lambda i: (0, 0, 0)
    moving = lambda i: (i, 0, 0)
    shapes = [jax.ShapeDtypeStruct((blocks, rows, LANES), bf16)]
    out_specs = [pl.BlockSpec((step, rows, LANES), moving)]
    if sums:
        shapes.append(jax.ShapeDtypeStruct((blocks, lines, LANES), f32))
        out_specs.append(pl.BlockSpec((step, lines, LANES), moving))
    return pl.pallas_call(
        functools.partial(mix_body, rows),
        out_shape=tuple(shapes),
        grid=(blocks // step,),
        in_specs=[
            pl.BlockSpec((step, rows, LANES), moving),
            pl.BlockSpec((step, lines, LANES), moving),
            pl.BlockSpec(gains.shape, whole),
            pl.BlockSpec(codes.shape, cube),
            pl.BlockSpec(unit.shape, cube),
        ],
        out_specs=tuple(out_specs),
        compiler_params=params(20),
        name="mix",
    )(x, inverse, gains, codes, unit)


def unpack_body(x_ref, o_ref):
    for head in range(x_ref.shape[0]):
        o_ref[:, head * LANES : (head + 1) * LANES] = x_ref[head]


def unpack(x):
    heads, rows, lanes = x.shape
    step = min(rows, 128)
    return pl.pallas_call(
        unpack_body,
        out_shape=jax.ShapeDtypeStruct((rows, heads * lanes), x.dtype),
        grid=(rows // step,),
        in_specs=[pl.BlockSpec((heads, step, lanes), lambda i: (0, i, 0))],
        out_specs=pl.BlockSpec((step, heads * lanes), lambda i: (i, 0)),
        compiler_params=params(20),
        name="unpack",
    )(x)


def passed_on(value, index, groups):
    def hop(source):
        return lambda sent: lax.ppermute(sent, "group", [(source, source + 1)])

    branches = [hop(source) for source in range(groups - 1)] + [lambda sent: sent]
    return lax.switch(index, branches, value)


def summed_over(value, axis):
    size = lax.axis_size(axis)
    bit = 1
    while bit < size:
        value = value + lax.ppermute(value, axis, [(i, i ^ bit) for i in range(size)])
        bit *= 2
    return value


def body(tokens, learning_rates, channel_gains, fast_init, step_size, update_table):
    groups = lax.axis_size("group")
    ranks = lax.axis_size("tok")
    me = lax.axis_index("group")
    rows, width = tokens.shape
    layers = fast_init.shape[0]
    lines = rows // LANES

    codes, unit, inverse_unit = setup(fast_init, groups)
    rates = learning_rates.reshape(layers, ranks, lines, LANES)
    stream = lax.all_to_all(pack(tokens), "tok", split_axis=0, concat_axis=0, tiled=True)
    inverse = None

    for layer in range(layers):
        chosen = slice(3 * layer, 3 * layer + 3)
        prepared = prep(stream, inverse, rates[layer], channel_gains[layer], rows)
        if inverse is None:
            inverse = prepared[2]
        early = pltpu.with_memory_space_constraint(prepared[0], pltpu.VMEM)
        late = prepared[1]
        flag = lax.dynamic_slice(update_table[layer], (me,), (1,))
        flag = jnp.where(me < groups - 1, flag, 0)
        step = step_size[layer]
        layer_unit, layer_inverse = unit[chosen], inverse_unit[chosen]

        def one(index, held):
            leaving, kept = lax.cond(
                index == me,
                lambda now, _: tick(flag, step, now, layer_unit, layer_inverse, early, late),
                lambda now, before: (now, before),
                *held,
            )
            return passed_on(leaving, index, groups), kept

        first = codes[chosen]
        _, entering = lax.fori_loop(jnp.maximum(me - 1, 0), me + 1, one, (first, first))
        last = layer + 1 == layers
        outcome = mix(stream, inverse, channel_gains[layer], entering, layer_unit, rows, not last)
        stream = outcome[0]
        if not last:
            inverse = lax.rsqrt(summed_over(outcome[1], "tok") / width + EPSILON)
    return unpack(lax.all_to_all(stream, "tok", split_axis=0, concat_axis=0, tiled=True))


def solution(mesh):
    in_specs = (
        P(("group", "tok"), None),
        P(None, "group"),
        P(None, None, "tok"),
        P(None, None, "tok", None, None),
        P(None, "tok"),
        P(),
    )
    out_specs = P(("group", "tok"), None)
    return jax.shard_map(body, mesh=mesh, in_specs=in_specs, out_specs=out_specs, check_vma=False)
```

time: 391 us -> 342 us (0.87); the launches traced: 394 us -> 338 us
  waiting for transfers between devices: 285 us -> 227 us
  local copies, waits for them, and re-layouts: 11.9 us -> 19.8 us
  starting transfers between devices: 14.5 us -> 21.9 us
  blocking collectives: 47.8 us -> 40.5 us
    ppermute x2, waiting for transfers between devices: 244 us -> 187 us  [hop(): return lambda sent: lax.ppermute(sent, 'group', [(source, source + 1)])]
    all_to_all x1 -> x0, blocking collectives: 13.5 us -> none  [body(): mine = jnp.sum(lax.all_to_all(partial, 'tok', 0, 0, tiled=True), axis=0)]
    ppermute x0 -> x4, starting transfers between devices: none -> 10.9 us  [summed_over(): lax.ppermute(value, axis, [(i, i ^ bit) for i in range(size)])]
    all_to_all x1 -> x0, waiting for transfers between devices: 9.38 us -> none  [body(): lax.all_to_all(jnp.broadcast_to(mine[None], (ranks, lines, LANES)), 'tok'...]
    ppermute x0 -> x4, waiting for transfers between devices: none -> 7.3 us  [summed_over(): lax.ppermute(value, axis, [(i, i ^ bit) for i in range(size)])]
    all_to_all x1, blocking collectives: 34.2 us -> 40.5 us  [body(): lax.all_to_all(stream, 'tok', split_axis=0, concat_axis=0, tiled=True)]
    pallas_call x2, Pallas kernels: 13.8 us -> 9.31 us  [prep(): pl.pallas_call(functools.partial(prep_body, inside, rows), out_shape=tupl...]
    unnamed x33 -> x32, local copies, waits for them, and re-layouts: 6.7 us -> 11 us
  transfers between devices with their start and end apart: 4 -> 7, of which waited for: 4 -> 7; matrix products, arithmetic and copies ran while one was open for 2% -> 1% of each run, Pallas kernels for 0% -> 0%
where the time goes in v2:
time: 342 us; the launch traced here: 338 us
  waiting for transfers between devices  227 us (66%)
  blocking collectives  40.5 us (12%)
  Pallas kernels  27.1 us (8%)
  starting transfers between devices  21.9 us (6%)
  local copies, waits for them, and re-layouts  19.8 us (6%)
    ppermute x2, waiting for transfers between devices, hop(): return lambda sent: lax.ppermute(sent, 'group', [(source, source + 1)])  187 us
    all_to_all x1, blocking collectives, body(): lax.all_to_all(stream, 'tok', split_axis=0, concat_axis=0, tiled=True)  40.5 us
    all_to_all x1, waiting for transfers between devices, body(): lax.all_to_all(pack(tokens), 'tok', split_axis=0, concat_axis=0, tiled=True)  32.9 us
    pallas_call x2, Pallas kernels, mix(): pl.pallas_call(functools.partial(mix_body, rows), out_shape=tuple(shapes)...  13.4 us
    unnamed x32, local copies, waits for them, and re-layouts  11 us
    ppermute x4, starting transfers between devices, summed_over(): lax.ppermute(value, axis, [(i, i ^ bit) for i in range(size)])  10.9 us
    pallas_call x2, Pallas kernels, prep(): pl.pallas_call(functools.partial(prep_body, inside, rows), out_shape=tupl...  9.31 us
    all_to_all x1, starting transfers between devices, body(): lax.all_to_all(pack(tokens), 'tok', split_axis=0, concat_axis=0, tiled=True)  8.46 us
  transfers between devices with their start and end apart: 7, of which 7 were waited for; matrix products, arithmetic and copies ran while one was open for 1% of the time, Pallas kernels for 0%

profile of v2, /device:TPU:120, one launch (start us, length us, event | category | flops | bytes accessed | tf_op | source)
XLA Modules:
  0.0 338.1 jit_solution(2894292829430640368)
XLA Ops:
  0.0 1.6 copy-done.6
  2.3 1.3 copy-done.3
  3.6 8.5 %all-to-all-start = ((bf16[16,528,128]{2,1,0:T(8,128)(2,1)}), bf16[16,528,128]{2,1,0:T(8,128)(2,1)S(1)}, u32[]{:S(2)}, u32[]{:S(2)}) async-start(bf16[16,528,128]{2,1,0:T(8,128)(2,1)} %copy-done.3), calls=%async_computation | async-start | bytes 4325376 | tf_op jit(solution)/shard_map/all_to_all | solution.py:394
  16.6 1.0 fusion.3
  17.5 32.9 %all-to-all-done.refs_0_.x_ref = bf16[16,528,128]{2,1,0:T(8,128)(2,1)S(1)} async-done(((bf16[16,528,128]{2,1,0:T(8,128)(2,1)}), bf16[16,528,128]{2,1,0:T(8,128)(2,1)S(1)}, u32[]{:S(2)}, u32[]{:S(2)}) %all-to-all-start) | async-done | bytes 2162720 | tf_op jit(solution)/shard_map/all_to_all | solution.py:394
  50.5 1.3 copy-done
  51.8 1.6 copy-done.1
  53.4 4.6 %prep.2 = (bf16[2,4096,128]{2,1,0:T(8,128)(2,1)S(1)}, bf16[2,4096,128]{2,1,0:T(8,128)(2,1)}, f32[16,4,128]{2,1,0:T(4,128)S(1)}) custom-call(bf16[16,528,128]{2,1,0:T(8,128)(2,1)S(1)} %copy-done.1, f32[16,4,128]{2,1,0:T(4,128)S(1)} %bitcast.16, f32[5,128]{1,0:T(8,128)S(1)} %bitcast.17), custom_call_target="tpu_custom_call" | custom-call | tf_op jit(solution)/shard_map/prep/pallas_call | solution.py:205
  58.0 174.8 %while.24 = (s32[]{:T(128)}, s16[3,128,128]{2,1,0:T(8,128)(2,1)S(1)}, s16[3,128,128]{2,1,0:T(8,128)(2,1)S(1)}, s32[]{:T(128)}, s32[]{:T(128)}, /*index=5*/s32[1]...) while((s32[]{:T(128)}, ...), condition=%wide.region_19.20_spmd, body=%wide.region_0.19_spmd.sunk | while | flops 5 | bytes 786739 | solution.py:419
  58.1 171.6 %conditional.9 = (s16[3,128,128]{2,1,0:T(8,128)(2,1)}) conditional(s32[]{:T(128)} %clamp.8, s16[3,128,128]{2,1,0:T(8,128)(2,1)S(1)} %get-tuple-element.468, s16[3,128,128]{2,1,0:T(8,128)(2,1)S(1)} %get-tuple-element.468, s16[3,128,128]{2,1,0:T(8,128)(2,1)S(1)} %get-tuple-element.468, ...), branch_computations={%region_3.3_spmd, %region_4.4_spmd, %region_5.5_spmd, %region_6.6_... | conditional | bytes 393264 | solution.py:372
  58.1 1.3 collective-permute-start.14
  59.4 170.2 %collective-permute-done.14 = s16[3,128,128]{2,1,0:T(8,128)(2,1)} collective-permute-done((s16[3,128,128]{2,1,0:T(8,128)(2,1)S(1)}, s16[3,128,128]{2,1,0:T(8,128)(2,1)}, u32[]{:S(2)}, u32[]{:S(2)}) %collective-permute-start.14) | collective-permute-done | bytes 98336 | tf_op jit(solution)/shard_map/while/body/cond/branch_14_fun/ppermute | solution.py:369
  229.7 0.9 copy.62
  232.8 1.6 copy-done.2
  234.4 7.7 %mix.2 = (bf16[16,512,128]{2,1,0:T(8,128)(2,1)S(1)}, f32[16,4,128]{2,1,0:T(4,128)S(1)}) custom-call(bf16[16,528,128]{2,1,0:T(8,128)(2,1)S(1)} %copy-done.2, f32[16,4,128]{2,1,0:T(4,128)S(1)} %get-tuple-element.265.inverse_ref, f32[5,128]{1,0:T(8,128)S(1)} %bitcast.18, s16[3,128,128]{2,1,0:T(8,128)(2,1)S(1)} %get-tuple-element.271.w_ref, ...), custom_call_target="tpu_custom_call" | custom-call | tf_op jit(solution)/shard_map/mix/pallas_call | solution.py:331
  242.2 1.2 collective-permute-done.30
  243.4 1.9 collective-permute-start.31
  245.3 2.2 collective-permute-done.31
  247.6 3.3 collective-permute-start.32
  250.9 2.2 collective-permute-done.32
  253.1 5.7 %collective-permute-start.33 = (f32[16,4,128]{2,1,0:T(4,128)S(1)}, f32[16,4,128]{2,1,0:T(4,128)S(1)}, u32[]{:S(2)}, u32[]{:S(2)}) collective-permute-start(f32[16,4,128]{2,1,0:T(4,128)S(1)} %add.37), channel_id=1, source_target_pairs={{0,8},{1,9},{2,10},{3,11},{4,12},{5,13},{6,14},{7,15},{8,0},{9,1},... | collective-permute-start | bytes 98312 | tf_op jit(solution)/shard_map/ppermute | solution.py:379
  259.4 1.6 collective-permute-done.33
  261.1 4.7 %prep.3 = (bf16[2,4096,128]{2,1,0:T(8,128)(2,1)S(1)}, bf16[2,4096,128]{2,1,0:T(8,128)(2,1)}) custom-call(bf16[16,512,128]{2,1,0:T(8,128)(2,1)S(1)} %get-tuple-element.272.refs_0_.x_ref, f32[16,4,128]{2,1,0:T(4,128)S(1)} %add_rsqrt_fusion.refs_1_.inverse_ref, f32[16,4,128]{2,1,0:T(4,128)S(1)} %bitcast.15, f32[5,128]{1,0:T(8,128)S(1)} %bitcast.19), custom_call_target="tpu_custom_call" | custom-call | tf_op jit(solution)/shard_map/prep/pallas_call | solution.py:205
  265.7 1.3 copy-done.4
  267.1 21.1 %while.25 = (s32[]{:T(128)}, s16[3,128,128]{2,1,0:T(8,128)(2,1)S(1)}, s16[3,128,128]{2,1,0:T(8,128)(2,1)S(1)}, s32[]{:T(128)}, s32[]{:T(128)}, /*index=5*/s32[1]...) while((s32[]{:T(128)}, ...), condition=%wide.region_39.40_spmd, body=%wide.region_20.39_spmd.sunk | while | flops 5 | bytes 786739 | solution.py:419
  267.1 17.9 %conditional.11 = (s16[3,128,128]{2,1,0:T(8,128)(2,1)}) conditional(s32[]{:T(128)} %clamp.9, s16[3,128,128]{2,1,0:T(8,128)(2,1)S(1)} %get-tuple-element.481, s16[3,128,128]{2,1,0:T(8,128)(2,1)S(1)} %get-tuple-element.481, s16[3,128,128]{2,1,0:T(8,128)(2,1)S(1)} %get-tuple-element.481, ...), branch_computations={%region_23.23_spmd, %region_24.24_spmd, %region_25.25_spmd, %regio... | conditional | bytes 393264 | solution.py:372
  267.1 1.3 collective-permute-start.29
  268.4 16.6 %collective-permute-done.29 = s16[3,128,128]{2,1,0:T(8,128)(2,1)} collective-permute-done((s16[3,128,128]{2,1,0:T(8,128)(2,1)S(1)}, s16[3,128,128]{2,1,0:T(8,128)(2,1)}, u32[]{:S(2)}, u32[]{:S(2)}) %collective-permute-start.29) | collective-permute-done | bytes 98336 | tf_op jit(solution)/shard_map/while/body/cond/branch_14_fun/ppermute | solution.py:369
  288.1 1.6 copy-done.5
  289.7 5.7 %mix.3 = bf16[16,512,128]{2,1,0:T(8,128)(2,1)S(1)} custom-call(bf16[16,512,128]{2,1,0:T(8,128)(2,1)S(1)} %copy-done.5, f32[16,4,128]{2,1,0:T(4,128)S(1)} %add_rsqrt_fusion.refs_1_.inverse_ref, f32[5,128]{1,0:T(8,128)S(1)} %bitcast.20, s16[3,128,128]{2,1,0:T(8,128)(2,1)S(1)} %get-tuple-element.276.w_ref, f32[3,128,128]{2,1,0:T(8,128)S(1)} %get-tuple-element.615), custom_call_target="tpu_custom_call" | custom-call | tf_op jit(solution)/shard_map/mix/pallas_call | solution.py:331
  295.4 40.5 %all_to_all.10.x_ref = bf16[16,512,128]{2,1,0:T(8,128)(2,1)S(1)} all-to-all(bf16[16,512,128]{2,1,0:T(8,128)(2,1)S(1)} %mix.3), channel_id=1, replica_groups=mesh['group'=16,'tok'=16] {'tok'}, dimensions={0} | all-to-all | bytes 4194304 | tf_op jit(solution)/shard_map/all_to_all | solution.py:425
  335.9 2.1 unpack.1
  (53 shorter events, 12.6 us)
Async XLA Ops:
  0.0 1.6 copy-start.6
  2.2 1.3 copy-start.3
  3.6 8.5 %copy-start.7 = (f32[2,3,1,128,128]{4,3,2,1,0:T(8,128)S(1)}, f32[2,3,1,128,128]{4,3,2,1,0:T(8,128)}, u32[]{:S(2)}) copy-start(f32[2,3,1,128,128]{4,3,2,1,0:T(8,128)} %param.49) | copy-start | bytes 1179652
  3.6 8.8 %copy-start.12 = (f32[2,5,128]{2,0,1:T(2,128)S(1)}, f32[2,5,128]{2,0,1:T(2,128)}, u32[]{:S(2)}) copy-start(f32[2,5,128]{2,0,1:T(2,128)} %param.48) | copy-start | bytes 15364
  3.6 11.5 %copy-start.13 = (f32[2,1]{0,1:T(1,128)S(1)}, f32[2,1]{0,1:T(1,128)}, u32[]{:S(2)}) copy-start(f32[2,1]{0,1:T(1,128)} %param.50) | copy-start | bytes 28
  3.6 46.9 %all-to-all-start = ((bf16[16,528,128]{2,1,0:T(8,128)(2,1)}), bf16[16,528,128]{2,1,0:T(8,128)(2,1)S(1)}, u32[]{:S(2)}, u32[]{:S(2)}) async-start(bf16[16,528,128]{2,1,0:T(8,128)(2,1)} %copy-done.3), calls=%async_computation | async-start | bytes 4325376 | tf_op jit(solution)/shard_map/all_to_all | solution.py:394
  16.6 41.5 %copy-start.11 = (s16[3,128,128]{2,1,0:T(8,128)(2,1)S(1)}, s16[3,128,128]{2,1,0:T(8,128)(2,1)}, u32[]{:S(2)}) copy-start(s16[3,128,128]{2,1,0:T(8,128)(2,1)} %copy.57) | copy-start | bytes 294916
  50.5 1.3 copy-start
  51.8 1.6 copy-start.1
  53.4 4.6 %copy-start.8 = (f32[3,128,128]{2,1,0:T(8,128)S(1)}, f32[3,128,128]{2,1,0:T(8,128)}, u32[]{:S(2)}) copy-start(f32[3,128,128]{2,1,0:T(8,128)} %get-tuple-element.498.unit_ref) | copy-start | bytes 589828
  53.4 4.6 %copy-start.10 = (f32[3,128,128]{2,1,0:T(8,128)S(1)}, f32[3,128,128]{2,1,0:T(8,128)}, u32[]{:S(2)}) copy-start(f32[3,128,128]{2,1,0:T(8,128)} %get-tuple-element.499) | copy-start | bytes 589828
  58.1 171.5 %collective-permute-start.14 = (s16[3,128,128]{2,1,0:T(8,128)(2,1)S(1)}, s16[3,128,128]{2,1,0:T(8,128)(2,1)}, u32[]{:S(2)}, u32[]{:S(2)}) collective-permute-start(s16[3,128,128]{2,1,0:T(8,128)(2,1)S(1)} %param.16), channel_id=1, source_target_pairs={{224,240},{225,241},{226,242},{227,243},{228,244},{229,245},{230,2... | collective-permute-start | bytes 294920 | tf_op jit(solution)/shard_map/while/body/cond/branch_14_fun/ppermute | solution.py:369
  232.8 1.6 copy-start.2
  234.4 32.6 %copy-start.9 = (f32[3,128,128]{2,1,0:T(8,128)S(1)}, f32[3,128,128]{2,1,0:T(8,128)}, u32[]{:S(2)}) copy-start(f32[3,128,128]{2,1,0:T(8,128)} %get-tuple-element.541) | copy-start | bytes 589828
  242.1 1.2 collective-permute-start.30
  243.4 4.2 %collective-permute-start.31 = (f32[16,4,128]{2,1,0:T(4,128)S(1)}, f32[16,4,128]{2,1,0:T(4,128)S(1)}, u32[]{:S(2)}, u32[]{:S(2)}) collective-permute-start(f32[16,4,128]{2,1,0:T(4,128)S(1)} %add.35), channel_id=1, source_target_pairs={{0,2},{1,3},{2,0},{3,1},{4,6},{5,7},{6,4},{7,5},{8,10},{9,11},{10,... | collective-permute-start | bytes 98312 | tf_op jit(solution)/shard_map/ppermute | solution.py:379
  247.6 5.5 %collective-permute-start.32 = (f32[16,4,128]{2,1,0:T(4,128)S(1)}, f32[16,4,128]{2,1,0:T(4,128)S(1)}, u32[]{:S(2)}, u32[]{:S(2)}) collective-permute-start(f32[16,4,128]{2,1,0:T(4,128)S(1)} %add.36), channel_id=1, source_target_pairs={{0,4},{1,5},{2,6},{3,7},{4,0},{5,1},{6,2},{7,3},{8,12},{9,13},{10,... | collective-permute-start | bytes 98312 | tf_op jit(solution)/shard_map/ppermute | solution.py:379
  253.1 7.9 %collective-permute-start.33 = (f32[16,4,128]{2,1,0:T(4,128)S(1)}, f32[16,4,128]{2,1,0:T(4,128)S(1)}, u32[]{:S(2)}, u32[]{:S(2)}) collective-permute-start(f32[16,4,128]{2,1,0:T(4,128)S(1)} %add.37), channel_id=1, source_target_pairs={{0,8},{1,9},{2,10},{3,11},{4,12},{5,13},{6,14},{7,15},{8,0},{9,1},... | collective-permute-start | bytes 98312 | tf_op jit(solution)/shard_map/ppermute | solution.py:379
  265.7 1.3 copy-start.4
  267.1 17.9 %collective-permute-start.29 = (s16[3,128,128]{2,1,0:T(8,128)(2,1)S(1)}, s16[3,128,128]{2,1,0:T(8,128)(2,1)}, u32[]{:S(2)}, u32[]{:S(2)}) collective-permute-start(s16[3,128,128]{2,1,0:T(8,128)(2,1)S(1)} %param.36), channel_id=1, source_target_pairs={{224,240},{225,241},{226,242},{227,243},{228,244},{229,245},{230,2... | collective-permute-start | bytes 294920 | tf_op jit(solution)/shard_map/while/body/cond/branch_14_fun/ppermute | solution.py:369
  288.1 1.6 copy-start.5

commit v3 on v2

--- a/solution.py
+++ b/solution.py
@@ -288,26 +288,27 @@
     weights = [decode(w_ref[j], unit_ref[j]).astype(bf16) for j in range(3)]
     gate_up = jnp.concatenate(weights[:2], axis=1)
     down = weights[2].T
-    norm, query, scale = gain_ref[0:1, :], gain_ref[1:2, :], gain_ref[4:5, :]
+    query, scale = gain_ref[0:1, :] * gain_ref[1:2, :], gain_ref[4:5, :]
     lines = rows // LANES
+    blocks = x_ref.shape[0]
+    pieces = []
+    for block in range(blocks):
+        inverse = column_of(inverse_ref[block])
+        for r in range(lines):
+            wide = x_ref[block, r * LANES : (r + 1) * LANES, :].astype(f32)
+            pieces.append((wide * inverse[:, r : r + 1] * query).astype(bf16))
+    both = dot(jnp.concatenate(pieces, axis=0), gate_up)
+    gate, up = both[:, :LANES], both[:, LANES:]
+    hidden = (gate * (0.5 * jnp.tanh(0.5 * gate) + 0.5) * up).astype(bf16)
+    output = dot(hidden, down)
     ones = jnp.ones((8, LANES), bf16)
-    for block in range(x_ref.shape[0]):
-        inverse = column_of(inverse_ref[block])
-        wide = x_ref[block].astype(f32)
-        pieces = [
-            (wide[r * LANES : (r + 1) * LANES] * inverse[:, r : r + 1] * norm * query).astype(bf16)
-            for r in range(lines)
-        ]
-        both = dot(jnp.concatenate(pieces, axis=0), gate_up)
-        gate, up = both[:, :LANES], both[:, LANES:]
-        hidden = (gate * (0.5 * jnp.tanh(0.5 * gate) + 0.5) * up).astype(bf16)
-        output = dot(hidden, down)
-        mixed = (wide + scale * output).astype(bf16)
+    turned = (((1,), (1,)), ((), ()))
+    for block in range(blocks):
+        mixed = (x_ref[block].astype(f32) + scale * output[block * rows : (block + 1) * rows]).astype(bf16)
         o_ref[block] = mixed
         if part_ref:
             square = mixed.astype(f32)
             high, low = two_parts(square * square)
-            turned = (((1,), (1,)), ((), ()))
             total = lax.dot_general(ones, high, turned, preferred_element_type=f32) + lax.dot_general(
                 ones, low, turned, preferred_element_type=f32
             )
@@ -365,11 +366,10 @@
 
 
 def passed_on(value, index, groups):
-    def hop(source):
-        return lambda sent: lax.ppermute(sent, "group", [(source, source + 1)])
-
-    branches = [hop(source) for source in range(groups - 1)] + [lambda sent: sent]
-    return lax.switch(index, branches, value)
+    def hop(target):
+        return lambda sent: lax.ppermute(sent, "group", [(target - 1, target)])
+
+    return lax.switch(index, [lambda sent: sent] + [hop(target) for target in range(1, groups)], value)
 
 
 def summed_over(value, axis):
@@ -396,6 +396,7 @@
 
     for layer in range(layers):
         chosen = slice(3 * layer, 3 * layer + 3)
+        stream = pltpu.with_memory_space_constraint(stream, pltpu.HBM)
         prepared = prep(stream, inverse, rates[layer], channel_gains[layer], rows)
         if inverse is None:
             inverse = prepared[2]
@@ -407,16 +408,17 @@
         layer_unit, layer_inverse = unit[chosen], inverse_unit[chosen]
 
         def one(index, held):
-            leaving, kept = lax.cond(
+            arrived = passed_on(held[0], index, groups)
+            return lax.cond(
                 index == me,
                 lambda now, _: tick(flag, step, now, layer_unit, layer_inverse, early, late),
                 lambda now, before: (now, before),
-                *held,
+                arrived,
+                held[1],
             )
-            return passed_on(leaving, index, groups), kept
 
         first = codes[chosen]
-        _, entering = lax.fori_loop(jnp.maximum(me - 1, 0), me + 1, one, (first, first))
+        _, entering = lax.fori_loop(me, jnp.minimum(me + 2, groups), one, (first, first))
         last = layer + 1 == layers
         outcome = mix(stream, inverse, channel_gains[layer], entering, layer_unit, rows, not last)
         stream = outcome[0]

time: 342 us -> 325 us (0.950)
  local copies, waits for them, and re-layouts: 19.8 us -> 4.38 us
  starting transfers between devices: 21.9 us -> 18.3 us
    unnamed x32 -> x18, local copies, waits for them, and re-layouts: 11 us -> 2.97 us
    ppermute x2, waiting for transfers between devices: 187 us -> 180 us  [hop(): return lambda sent: lax.ppermute(sent, 'group', [(target - 1, target)])]
    ppermute x4, starting transfers between devices: 10.9 us -> 7.18 us  [summed_over(): lax.ppermute(value, axis, [(i, i ^ bit) for i in range(size)])]
    ppermute x4, waiting for transfers between devices: 7.3 us -> 11 us  [summed_over(): lax.ppermute(value, axis, [(i, i ^ bit) for i in range(size)])]
    while x4 -> x0, local copies, waits for them, and re-layouts: 3.57 us -> none
  transfers between devices with their start and end apart: 7 -> 7, of which waited for: 7 -> 7; matrix products, arithmetic and copies ran while one was open for 1% -> 0% of each run, Pallas kernels for 0% -> 0%
where the time goes in v3:
time: 325 us; the launch traced here: 320 us
  waiting for transfers between devices  227 us (70%)
  blocking collectives  39.4 us (12%)
  Pallas kernels  30 us (9%)
  starting transfers between devices  18.3 us (6%)
  local copies, waits for them, and re-layouts  4.38 us (1%)
    ppermute x2, waiting for transfers between devices, hop(): return lambda sent: lax.ppermute(sent, 'group', [(target - 1, target)])  180 us
    all_to_all x1, blocking collectives, body(): lax.all_to_all(stream, 'tok', split_axis=0, concat_axis=0, tiled=True)  39.4 us
    all_to_all x1, waiting for transfers between devices, body(): lax.all_to_all(pack(tokens), 'tok', split_axis=0, concat_axis=0, tiled=True)  36 us
    pallas_call x2, Pallas kernels, mix(): pl.pallas_call(functools.partial(mix_body, rows), out_shape=tuple(shapes)...  12.5 us
    pallas_call x2, Pallas kernels, prep(): pl.pallas_call(functools.partial(prep_body, inside, rows), out_shape=tupl...  11.9 us
    ppermute x4, waiting for transfers between devices, summed_over(): lax.ppermute(value, axis, [(i, i ^ bit) for i in range(size)])  11 us
    all_to_all x1, starting transfers between devices, body(): lax.all_to_all(pack(tokens), 'tok', split_axis=0, concat_axis=0, tiled=True)  8.52 us
    ppermute x4, starting transfers between devices, summed_over(): lax.ppermute(value, axis, [(i, i ^ bit) for i in range(size)])  7.18 us
  transfers between devices with their start and end apart: 7, of which 7 were waited for; matrix products, arithmetic and copies ran while one was open for 0% of the time, Pallas kernels for 0%

profile of v3, /device:TPU:120, one launch (start us, length us, event | category | flops | bytes accessed | tf_op | source)
XLA Modules:
  0.0 320.5 jit_solution(12516432113934310802)
XLA Ops:
  0.0 1.6 copy-done.1
  1.6 2.0 pack.1
  3.6 8.5 %all-to-all-start = ((bf16[16,528,128]{2,1,0:T(8,128)(2,1)}), bf16[16,528,128]{2,1,0:T(8,128)(2,1)}, u32[]{:S(2)}, u32[]{:S(2)}) async-start(bf16[16,528,128]{2,1,0:T(8,128)(2,1)} %pack.1), calls=%async_computation | async-start | bytes 4325376 | tf_op jit(solution)/shard_map/all_to_all | solution.py:394
  12.6 0.7 constant_dynamic-slice_fusion
  13.9 0.6 fusion.6
  14.6 36.0 %all-to-all-done.refs_0_.x_ref = bf16[16,528,128]{2,1,0:T(8,128)(2,1)} async-done(((bf16[16,528,128]{2,1,0:T(8,128)(2,1)}), bf16[16,528,128]{2,1,0:T(8,128)(2,1)}, u32[]{:S(2)}, u32[]{:S(2)}) %all-to-all-start) | async-done | bytes 2162720 | tf_op jit(solution)/shard_map/all_to_all | solution.py:394
  50.6 5.9 %prep.2 = (bf16[2,4096,128]{2,1,0:T(8,128)(2,1)S(1)}, bf16[2,4096,128]{2,1,0:T(8,128)(2,1)}, f32[16,4,128]{2,1,0:T(4,128)S(1)}) custom-call(bf16[16,528,128]{2,1,0:T(8,128)(2,1)} %all-to-all-done.refs_0_.x_ref, f32[16,4,128]{2,1,0:T(4,128)S(1)} %bitcast.16, f32[5,128]{1,0:T(8,128)S(1)} %bitcast.17), custom_call_target="tpu_custom_call" | custom-call | tf_op jit(solution)/shard_map/prep/pallas_call | solution.py:205
  56.5 173.0 %while.120 = (s32[]{:T(128)}, s16[3,128,128]{2,1,0:T(8,128)(2,1)S(1)}, s16[3,128,128]{2,1,0:T(8,128)(2,1)S(1)}, s32[]{:T(128)}, s32[]{:T(128)}, /*index=5*/s32[1...) while((s32[]{:T(128)}, ...), condition=%wide.region_19.20_spmd, body=%wide.region_0.19_spmd.sunk | while | flops 5 | bytes 786723 | solution.py:421
  56.5 172.3 %conditional.8 = (s16[3,128,128]{2,1,0:T(8,128)(2,1)S(1)}) conditional(s32[]{:T(128)} %clamp.8, s16[3,128,128]{2,1,0:T(8,128)(2,1)S(1)} %get-tuple-element.492, s16[3,128,128]{2,1,0:T(8,128)(2,1)S(1)} %get-tuple-element.492, s16[3,128,128]{2,1,0:T(8,128)(2,1)S(1)} %get-tuple-element.492, ...), branch_computations={%region_1.1_spmd, %region_2.2_spmd, %region_3.3_spmd, %region_4.4_... | conditional | bytes 589872 | solution.py:372
  56.5 1.3 collective-permute-start.14
  57.8 171.0 %collective-permute-done.14 = s16[3,128,128]{2,1,0:T(8,128)(2,1)S(1)} collective-permute-done((s16[3,128,128]{2,1,0:T(8,128)(2,1)S(1)}, s16[3,128,128]{2,1,0:T(8,128)(2,1)S(1)}, u32[]{:S(2)}, u32[]{:S(2)}) %collective-permute-start.14) | collective-permute-done | bytes 98336 | tf_op jit(solution)/shard_map/while/body/cond/branch_15_fun/ppermute | solution.py:370
  228.8 0.7 conditional.9
  228.8 0.7 tick.2
  229.5 7.1 %mix.2 = (bf16[16,512,128]{2,1,0:T(8,128)(2,1)S(1)}, f32[16,4,128]{2,1,0:T(4,128)S(1)}) custom-call(bf16[16,528,128]{2,1,0:T(8,128)(2,1)} %all-to-all-done.refs_0_.x_ref, f32[16,4,128]{2,1,0:T(4,128)S(1)} %get-tuple-element.251.inverse_ref, f32[5,128]{1,0:T(8,128)S(1)} %bitcast.18, s16[3,128,128]{2,1,0:T(8,128)(2,1)S(1)} %get-tuple-element.257.w_ref, ...), custom_call_target="tpu_custom_call" | custom-call | tf_op jit(solution)/shard_map/mix/pallas_call | solution.py:332
  236.6 1.3 copy-done
  237.9 1.2 collective-permute-done.30
  239.1 0.5 collective-permute-start.31
  239.7 3.7 %collective-permute-done.31 = f32[16,4,128]{2,1,0:T(4,128)S(1)} collective-permute-done((f32[16,4,128]{2,1,0:T(4,128)S(1)}, f32[16,4,128]{2,1,0:T(4,128)S(1)}, u32[]{:S(2)}, u32[]{:S(2)}) %collective-permute-start.31) | collective-permute-done | bytes 32800 | tf_op jit(solution)/shard_map/ppermute | solution.py:379
  243.3 2.4 collective-permute-start.32
  245.8 3.1 collective-permute-done.32
  248.9 4.2 %collective-permute-start.33 = (f32[16,4,128]{2,1,0:T(4,128)S(1)}, f32[16,4,128]{2,1,0:T(4,128)S(1)}, u32[]{:S(2)}, u32[]{:S(2)}) collective-permute-start(f32[16,4,128]{2,1,0:T(4,128)S(1)} %add.36), channel_id=1, source_target_pairs={{0,8},{1,9},{2,10},{3,11},{4,12},{5,13},{6,14},{7,15},{8,0},{9,1},... | collective-permute-start | bytes 98312 | tf_op jit(solution)/shard_map/ppermute | solution.py:379
  253.8 3.0 collective-permute-done.33
  256.8 6.0 %prep.3 = (bf16[2,4096,128]{2,1,0:T(8,128)(2,1)S(1)}, bf16[2,4096,128]{2,1,0:T(8,128)(2,1)}) custom-call(bf16[16,512,128]{2,1,0:T(8,128)(2,1)} %copy-done, f32[16,4,128]{2,1,0:T(4,128)S(1)} %add_rsqrt_fusion.refs_1_.inverse_ref, f32[16,4,128]{2,1,0:T(4,128)S(1)} %bitcast.15, f32[5,128]{1,0:T(8,128)S(1)} %bitcast.19), custom_call_target="tpu_custom_call" | custom-call | tf_op jit(solution)/shard_map/prep/pallas_call | solution.py:205
  262.8 10.7 %while.121 = (s32[]{:T(128)}, s16[3,128,128]{2,1,0:T(8,128)(2,1)S(1)}, s16[3,128,128]{2,1,0:T(8,128)(2,1)S(1)}, s32[]{:T(128)}, s32[]{:T(128)}, /*index=5*/s32[1...) while((s32[]{:T(128)}, ...), condition=%wide.region_39.40_spmd, body=%wide.region_20.39_spmd.sunk | while | flops 5 | bytes 786723 | solution.py:421
  262.8 10.1 %conditional.10 = (s16[3,128,128]{2,1,0:T(8,128)(2,1)S(1)}) conditional(s32[]{:T(128)} %clamp.9, s16[3,128,128]{2,1,0:T(8,128)(2,1)S(1)} %get-tuple-element.534, s16[3,128,128]{2,1,0:T(8,128)(2,1)S(1)} %get-tuple-element.534, s16[3,128,128]{2,1,0:T(8,128)(2,1)S(1)} %get-tuple-element.534, ...), branch_computations={%region_21.21_spmd, %region_22.22_spmd, %region_23.23_spmd, %regio... | conditional | bytes 589872 | solution.py:372
  262.8 1.3 collective-permute-start.29
  264.1 8.8 %collective-permute-done.29 = s16[3,128,128]{2,1,0:T(8,128)(2,1)S(1)} collective-permute-done((s16[3,128,128]{2,1,0:T(8,128)(2,1)S(1)}, s16[3,128,128]{2,1,0:T(8,128)(2,1)S(1)}, u32[]{:S(2)}, u32[]{:S(2)}) %collective-permute-start.29) | collective-permute-done | bytes 98336 | tf_op jit(solution)/shard_map/while/body/cond/branch_15_fun/ppermute | solution.py:370
  272.8 0.6 conditional.11
  272.9 0.6 tick.3
  273.5 5.4 %mix.3 = bf16[16,512,128]{2,1,0:T(8,128)(2,1)S(1)} custom-call(bf16[16,512,128]{2,1,0:T(8,128)(2,1)} %copy-done, f32[16,4,128]{2,1,0:T(4,128)S(1)} %add_rsqrt_fusion.refs_1_.inverse_ref, f32[5,128]{1,0:T(8,128)S(1)} %bitcast.20, s16[3,128,128]{2,1,0:T(8,128)(2,1)S(1)} %get-tuple-element.262.w_ref, f32[3,128,128]{2,1,0:T(8,128)S(1)} %get-tuple-element.566), custom_call_target="tpu_custom_call" | custom-call | tf_op jit(solution)/shard_map/mix/pallas_call | solution.py:332
  279.0 39.4 %all_to_all.10.x_ref = bf16[16,512,128]{2,1,0:T(8,128)(2,1)S(1)} all-to-all(bf16[16,512,128]{2,1,0:T(8,128)(2,1)S(1)} %mix.3), channel_id=1, replica_groups=mesh['group'=16,'tok'=16] {'tok'}, dimensions={0} | all-to-all | bytes 4194304 | tf_op jit(solution)/shard_map/all_to_all | solution.py:427
  318.3 2.1 unpack.1
  (31 shorter events, 0.5 us)
Async XLA Ops:
  0.0 1.6 copy-start.1
  3.6 8.6 %copy-start.2 = (f32[2,3,1,128,128]{4,3,2,1,0:T(8,128)S(1)}, f32[2,3,1,128,128]{4,3,2,1,0:T(8,128)}, u32[]{:S(2)}) copy-start(f32[2,3,1,128,128]{4,3,2,1,0:T(8,128)} %param.49) | copy-start | bytes 1179652
  3.6 8.8 %copy-start.4 = (f32[2,5,128]{2,0,1:T(2,128)S(1)}, f32[2,5,128]{2,0,1:T(2,128)}, u32[]{:S(2)}) copy-start(f32[2,5,128]{2,0,1:T(2,128)} %param.48) | copy-start | bytes 15364
  3.6 8.9 %copy-start.6 = (s32[2,16]{1,0:T(2,128)S(1)}, s32[2,16]{1,0:T(2,128)}, u32[]{:S(2)}) copy-start(s32[2,16]{1,0:T(2,128)} %param.51) | copy-start | bytes 388
  3.6 10.2 %copy-start.5 = (f32[2,1]{0,1:T(1,128)S(1)}, f32[2,1]{0,1:T(1,128)}, u32[]{:S(2)}) copy-start(f32[2,1]{0,1:T(1,128)} %param.50) | copy-start | bytes 28
  3.6 47.0 %all-to-all-start = ((bf16[16,528,128]{2,1,0:T(8,128)(2,1)}), bf16[16,528,128]{2,1,0:T(8,128)(2,1)}, u32[]{:S(2)}, u32[]{:S(2)}) async-start(bf16[16,528,128]{2,1,0:T(8,128)(2,1)} %pack.1), calls=%async_computation | async-start | bytes 4325376 | tf_op jit(solution)/shard_map/all_to_all | solution.py:394
  12.2 2.4 copy-start.3
  56.5 172.3 %collective-permute-start.14 = (s16[3,128,128]{2,1,0:T(8,128)(2,1)S(1)}, s16[3,128,128]{2,1,0:T(8,128)(2,1)S(1)}, u32[]{:S(2)}, u32[]{:S(2)}) collective-permute-start(s16[3,128,128]{2,1,0:T(8,128)(2,1)S(1)} %param.15), channel_id=1, source_target_pairs={{224,240},{225,241},{226,242},{227,243},{228,244},{229,245},{230,2... | collective-permute-start | bytes 294920 | tf_op jit(solution)/shard_map/while/body/cond/branch_15_fun/ppermute | solution.py:370
  236.6 1.3 copy-start
  237.9 1.2 collective-permute-start.30
  239.1 4.2 %collective-permute-start.31 = (f32[16,4,128]{2,1,0:T(4,128)S(1)}, f32[16,4,128]{2,1,0:T(4,128)S(1)}, u32[]{:S(2)}, u32[]{:S(2)}) collective-permute-start(f32[16,4,128]{2,1,0:T(4,128)S(1)} %add.34), channel_id=1, source_target_pairs={{0,2},{1,3},{2,0},{3,1},{4,6},{5,7},{6,4},{7,5},{8,10},{9,11},{10,... | collective-permute-start | bytes 98312 | tf_op jit(solution)/shard_map/ppermute | solution.py:379
  243.3 5.5 %collective-permute-start.32 = (f32[16,4,128]{2,1,0:T(4,128)S(1)}, f32[16,4,128]{2,1,0:T(4,128)S(1)}, u32[]{:S(2)}, u32[]{:S(2)}) collective-permute-start(f32[16,4,128]{2,1,0:T(4,128)S(1)} %add.35), channel_id=1, source_target_pairs={{0,4},{1,5},{2,6},{3,7},{4,0},{5,1},{6,2},{7,3},{8,12},{9,13},{10,... | collective-permute-start | bytes 98312 | tf_op jit(solution)/shard_map/ppermute | solution.py:379
  248.9 7.9 %collective-permute-start.33 = (f32[16,4,128]{2,1,0:T(4,128)S(1)}, f32[16,4,128]{2,1,0:T(4,128)S(1)}, u32[]{:S(2)}, u32[]{:S(2)}) collective-permute-start(f32[16,4,128]{2,1,0:T(4,128)S(1)} %add.36), channel_id=1, source_target_pairs={{0,8},{1,9},{2,10},{3,11},{4,12},{5,13},{6,14},{7,15},{8,0},{9,1},... | collective-permute-start | bytes 98312 | tf_op jit(solution)/shard_map/ppermute | solution.py:379
  262.8 10.1 %collective-permute-start.29 = (s16[3,128,128]{2,1,0:T(8,128)(2,1)S(1)}, s16[3,128,128]{2,1,0:T(8,128)(2,1)S(1)}, u32[]{:S(2)}, u32[]{:S(2)}) collective-permute-start(s16[3,128,128]{2,1,0:T(8,128)(2,1)S(1)} %param.35), channel_id=1, source_target_pairs={{224,240},{225,241},{226,242},{227,243},{228,244},{229,245},{230,2... | collective-permute-start | bytes 294920 | tf_op jit(solution)/shard_map/while/body/cond/branch_15_fun/ppermute | solution.py:370
